TPU v7x, 128 devices: a whole 4x4x4 slice. The times are simulated.
128 devices in a mesh: gx: 16 (over x_hi, z, core), gy: 8 (over x_lo, y).
Axes of the slice: x: 4 (x_hi: 2, x_lo: 2; x = x_hi * 2 + x_lo), y: 4, z: 4, core: 2. Of those that a mesh axis runs over, the one named last changes fastest.
Arguments:
- populations: float32 [19, 256, 128, 128], P(None, 'gx', 'gy')
- panels: bfloat16 [64, 200, 128], P(None, None, ('gx', 'gy')), may hold values from -0.59765625 to 0.59765625
- modal_vel: bfloat16 [64, 2, 200], replicated, may hold values from -0.4375 to 0.4375
- marker_x: int32 [16, 8, 512], P('gx', 'gy'), may hold values from 0 to 15
- marker_y: int32 [16, 8, 512], P('gx', 'gy'), may hold values from 0 to 15
- marker_z: int32 [16, 8, 512], P('gx', 'gy'), may hold values from 0 to 127
- marker_riser: int32 [16, 8, 512], P('gx', 'gy'), may hold values from 0 to 63
Outputs:
- next_populations: float32 [19, 256, 128, 128], P(None, 'gx', 'gy')
- marker_force: float32 [16, 8, 3, 512], P('gx', 'gy')
- force_field: float32 [3, 256, 128, 128], P(None, 'gx', 'gy')
All inputs are finite; a program needn't handle non-finite values.
Results may differ from a plain program's by a relative error of at most 0.0008.
Values may be sent and summed in bfloat16 or wider, within the bound.
No kernel may reach another device: no remote copies, remote signals or barrier semaphores. Data moves between devices by JAX's collectives and lax.ppermute only.
A program may use at most 128 MiB of HBM per device.

v0:
```python
import jax
import jax.numpy as jnp
from jax import lax
from jax.experimental import pallas as pl
from jax.experimental.pallas import tpu as pltpu
from jax.sharding import PartitionSpec as P

VELOCITY = (
    (0, 0, 0),
    (1, 0, 0),
    (-1, 0, 0),
    (0, 1, 0),
    (0, -1, 0),
    (0, 0, 1),
    (0, 0, -1),
    (1, 1, 0),
    (-1, -1, 0),
    (1, -1, 0),
    (-1, 1, 0),
    (1, 0, 1),
    (-1, 0, -1),
    (1, 0, -1),
    (-1, 0, 1),
    (0, 1, 1),
    (0, -1, -1),
    (0, 1, -1),
    (0, -1, 1),
)
WEIGHT = (1.0 / 3.0,) + (1.0 / 18.0,) * 6 + (1.0 / 36.0,) * 12
RELAX = 0.8
CELLS = 16
DEPTH = 128
MARKS = 512
RISERS = 64
FRAME = 24


def slabs(axis, toward):
    order = []
    for layer in (1, 2, 3):
        for index in range(19):
            if VELOCITY[index][axis] * toward >= layer - 2:
                order.append((layer, index))
    return order


ORDER = {(axis, toward): slabs(axis, toward) for axis in (0, 1) for toward in (1, -1)}
PLACE = {key: {slab: k for k, slab in enumerate(order)} for key, order in ORDER.items()}
SLABS = len(ORDER[0, 1])
INWARD = {toward: [i for i in range(19) if VELOCITY[i][1] == toward] for toward in (1, -1)}


def near(layer, toward):
    return CELLS - layer if toward == 1 else layer - 1


def encode(value, index):
    return (value - WEIGHT[index]).astype(jnp.bfloat16)


def decode(value, index):
    return value.astype(jnp.float32) + WEIGHT[index]


def split(value):
    high = value.astype(jnp.bfloat16)
    low = (value - high.astype(jnp.float32)).astype(jnp.bfloat16)
    return high, low


def pack_faces(
    cells_far,
    mx_far,
    my_far,
    mz_far,
    riser_far,
    panel_far,
    modal_far,
    xup,
    xdown,
    yup,
    ydown,
    rows,
    cells,
    mx,
    my,
    mz,
    riser,
    panel,
    modal,
    marks,
    pairs,
    sems,
):
    copies = [
        pltpu.make_async_copy(far, here, sems.at[n])
        for n, (far, here) in enumerate(
            (
                (modal_far, modal),
                (panel_far, panel),
                (mx_far, mx),
                (my_far, my),
                (mz_far, mz),
                (riser_far, riser),
                (cells_far, cells),
            )
        )
    ]
    for copy in copies:
        copy.start()
    for copy in copies[:6]:
        copy.wait()
    for attr, source in enumerate((mx, my, mz, riser)):
        for n in range(4):
            marks[attr * 4 + n : attr * 4 + n + 1, :] = source[:, n * 128 : (n + 1) * 128].astype(
                jnp.float32
            )
    for n in range(RISERS):
        both = modal[n].astype(jnp.float32)
        for d in range(2):
            pairs[d * RISERS + n : d * RISERS + n + 1, :] = both[d : d + 1]
    product = lax.dot_general(
        panel[...],
        pairs[...].astype(jnp.bfloat16),
        (((1,), (1,)), ((), ())),
        preferred_element_type=jnp.float32,
    )
    mine = lax.broadcasted_iota(jnp.int32, product.shape, 0) == (
        lax.broadcasted_iota(jnp.int32, product.shape, 1) & (RISERS - 1)
    )
    row = jnp.sum(jnp.where(mine, product, 0.0), axis=0, keepdims=True)
    rows[...] = jnp.broadcast_to(row, rows.shape)
    copies[6].wait()
    for out, toward in ((xup, 1), (xdown, -1)):
        for k, (layer, index) in enumerate(ORDER[0, toward]):
            first = near(layer, toward) * CELLS
            out[k] = encode(cells[index, first : first + CELLS, :], index)
        out[SLABS] = marks[...].astype(jnp.bfloat16)
    for out, toward in ((yup, 1), (ydown, -1)):
        for k, (layer, index) in enumerate(ORDER[1, toward]):
            row = near(layer, toward)
            out[k] = encode(cells[index, pl.ds(row, CELLS, stride=CELLS), :], index)
        out[SLABS] = marks[...].astype(jnp.bfloat16)


def pack_corners(xlow, xhigh, yup, ydown, low, high):
    low[...] = xlow[...].astype(jnp.float32)
    high[...] = xhigh[...].astype(jnp.float32)
    place = lax.broadcasted_iota(jnp.int32, (8, DEPTH), 0)
    for out, toward in ((yup, 1), (ydown, -1)):
        for k, (layer, index) in enumerate(ORDER[1, toward]):
            row = near(layer, toward)
            tile = jnp.zeros((8, DEPTH), jnp.float32)
            for depth in (1, 2, 3):
                for source, side, at in ((high, -1, depth - 1), (low, 1, 8 - depth)):
                    slot = PLACE[0, side].get((depth, index))
                    if slot is not None:
                        tile = jnp.where(place == at, source[slot, row : row + 1, :], tile)
            out[k] = tile.astype(jnp.bfloat16)
        for n, source in enumerate((low, high)):
            for half in range(2):
                out[SLABS + 2 * n + half] = source[SLABS, 8 * half : 8 * half + 8, :].astype(
                    jnp.bfloat16
                )


def moments(reads):
    density = None
    momentum = [None, None, None]
    for index, value in enumerate(reads):
        density = value if density is None else density + value
        for axis in range(3):
            sign = VELOCITY[index][axis]
            if sign == 1:
                momentum[axis] = value if momentum[axis] is None else momentum[axis] + value
            elif sign == -1:
                momentum[axis] = -value if momentum[axis] is None else momentum[axis] - value
    return density, momentum


def along(vector, direction):
    total = None
    for axis in range(3):
        if direction[axis] == 1:
            total = vector[axis] if total is None else total + vector[axis]
        elif direction[axis] == -1:
            total = -vector[axis] if total is None else total - vector[axis]
    return total


def spin(value, shift, axis):
    return pltpu.roll(value, shift % value.shape[axis], axis) if shift else value


def step_kernel(
    cells,
    xlow,
    xhigh,
    ylow,
    yhigh,
    clow,
    chigh,
    own_x,
    own_y,
    own_z,
    own_riser,
    table,
    nxt,
    push,
    field,
    wide,
    edge,
    strip,
    lines,
    vel,
    tall,
    smooth,
    dens,
    impulse,
    sem,
):
    inner = pltpu.make_async_copy(cells, wide.at[:, pl.ds(0, CELLS * CELLS), :], sem)
    inner.start()
    f32 = jnp.float32
    for message, toward in ((xlow, 1), (xhigh, -1)):
        for k, (layer, index) in enumerate(ORDER[0, toward]):
            column = FRAME - layer if toward == 1 else CELLS - 1 + layer
            wide[index, column * CELLS : (column + 1) * CELLS, :] = decode(message[k], index)

    def frame(face, corner, k, index):
        return jnp.concatenate([decode(face[k], index), decode(corner[k], index)], axis=0)

    inner.wait()

    for s, (toward, face, corner) in enumerate(((1, ylow, clow), (-1, yhigh, chigh))):
        first = 0 if toward == 1 else CELLS - 1
        for n, index in enumerate(INWARD[toward]):
            edge[s, n] = frame(face, corner, PLACE[1, toward][1, index], index)
        for layer in (1, 2):

            def reads():
                for index in range(19):
                    cx, cy, cz = VELOCITY[index]
                    source = layer + toward * cy
                    if source == 0:
                        value = wide[index, pl.ds(first, FRAME, stride=CELLS), :]
                    else:
                        value = frame(face, corner, PLACE[1, toward][source, index], index)
                    yield spin(spin(value, cx, 0), cz, 1)

            density, momentum = moments(reads())
            for axis in range(3):
                strip[s, layer - 1, axis] = momentum[axis] / density

    row = lax.broadcasted_iota(jnp.int32, (CELLS, DEPTH), 0)

    def column(j, keep):
        def reads():
            for index in range(19):
                cx, cy, cz = VELOCITY[index]
                at = lax.rem(j + (FRAME - 2) - cx, FRAME)
                value = wide[index, pl.ds(pl.multiple_of(at * CELLS, CELLS), CELLS), :]
                if cy:
                    s = 0 if cy == 1 else 1
                    n = INWARD[cy].index(index)
                    line = edge[s, n, pl.ds(at, 1), :]
                    value = jnp.where(row == (0 if cy == 1 else CELLS - 1), line, spin(value, cy, 0))
                value = spin(value, cz, 1)
                if keep:
                    nxt[index, pl.ds(pl.multiple_of((j - 2) * CELLS, CELLS), CELLS), :] = value
                yield value

        density, momentum = moments(reads())
        if keep:
            dens[0, j - 2] = density
        for axis in range(3):
            speed = momentum[axis] / density
            if keep:
                dens[1 + axis, j - 2] = momentum[axis]
            vel[axis, j] = speed
            at = pl.ds(lax.rem(j + 22, FRAME), 1)
            lines[0, axis, at, :] = speed[0:1]
            lines[1, axis, at, :] = speed[CELLS - 1 : CELLS]

    for j in (0, 1, 18, 19):
        column(jnp.int32(j), False)

    @pl.loop(2, 18)
    def _(j):
        column(j, True)

    @pl.loop(0, 20)
    def _(j):
        at = pl.ds(lax.rem(j + 22, FRAME), 1)
        for axis in range(3):
            value = vel[axis, j]
            before = jnp.where(row == 0, strip[0, 0, axis, at, :], spin(value, 1, 0))
            after = jnp.where(row == CELLS - 1, strip[1, 0, axis, at, :], spin(value, -1, 0))
            tall[axis, j] = 0.5 * value + 0.25 * (before + after)

    @pl.loop(0, 18)
    def _(j):
        for axis in range(3):
            smooth[axis, j] = 0.5 * tall[axis, j + 1] + 0.25 * (tall[axis, j] + tall[axis, j + 2])

    place = lax.broadcasted_iota(jnp.int32, (FRAME, DEPTH), 0)
    inside = (place <= CELLS) | (place == FRAME - 1)
    rim = []
    for s in range(2):
        for axis in range(3):
            value = 0.5 * strip[s, 0, axis] + 0.25 * (strip[s, 1, axis] + lines[s, axis])
            value = 0.5 * value + 0.25 * (spin(value, 1, 0) + spin(value, -1, 0))
            rim.append(jnp.where(inside, value, 0.0))

    goal = split(table[...].T)
    goal = jnp.concatenate(goal, axis=1)

    def group(slab, chunks):
        return [
            jnp.concatenate(
                [slab[attr * 4 + n : attr * 4 + n + 1, :] for n in range(chunks)], axis=1
            )
            for attr in range(4)
        ]

    def hot(position, count):
        shape = (count, position.shape[1])
        return lax.broadcasted_iota(jnp.int32, shape, 0).astype(f32) == position

    def force_of(velocity, weight, z, riser):
        at_z = jnp.where(hot(z, DEPTH), 1.0, 0.0).astype(jnp.bfloat16)
        twice = jnp.concatenate([at_z, at_z], axis=0)
        picked = jnp.dot(goal, twice, preferred_element_type=f32)
        at_riser = hot(riser, RISERS)
        out = []
        for axis in range(3):
            both = jnp.concatenate(split(velocity[axis]), axis=1)
            speed = jnp.dot(both, twice, preferred_element_type=f32)
            sampled = jnp.sum(jnp.where(weight, speed, 0.0), axis=0, keepdims=True)
            if axis < 2:
                some = picked[axis * RISERS : (axis + 1) * RISERS]
                wanted = jnp.sum(jnp.where(at_riser, some, 0.0), axis=0, keepdims=True)
                out.append(2.0 * (wanted - sampled))
            else:
                out.append(-2.0 * sampled)
        return at_z, out

    contract = (((1,), (1,)), ((), ()))

    def spread(weight, at_z, force):
        parts = []
        for axis in range(3):
            parts.append(jnp.where(weight, force[axis], 0.0))
        high, low = split(jnp.concatenate(parts, axis=0))
        both = jnp.concatenate([high, low], axis=1)
        twice = jnp.concatenate([at_z, at_z], axis=1)
        return lax.dot_general(both, twice, contract, preferred_element_type=f32)

    mx, my, mz, riser = (m[...].astype(f32) for m in (own_x, own_y, own_z, own_riser))
    weight = hot(mx * CELLS + my, CELLS * CELLS)
    velocity = [smooth[axis, 1 : CELLS + 1].reshape(CELLS * CELLS, DEPTH) for axis in range(3)]
    at_z, force = force_of(velocity, weight, mz, riser)
    for axis in range(3):
        push[axis] = force[axis]
    at_cell = jnp.where(weight, 1.0, 0.0).astype(jnp.bfloat16)
    where_z = hot(mz, DEPTH)
    for axis in range(3):
        high, low = split(jnp.where(where_z, force[axis], 0.0))
        got = lax.dot_general(at_cell, high, contract, preferred_element_type=f32)
        got = got + lax.dot_general(at_cell, low, contract, preferred_element_type=f32)
        impulse[axis, 1 : CELLS + 1] = got.reshape(CELLS, CELLS, DEPTH)
    for message, at, spot in ((xlow, CELLS - 1, 0), (xhigh, 0, CELLS + 1)):
        mx, my, mz, riser = group(message[SLABS].astype(f32), 4)
        weight = hot(jnp.where(mx == at, my, -1.0), CELLS)
        at_z, force = force_of([smooth[axis, spot] for axis in range(3)], weight, mz, riser)
        got = spread(weight, at_z, force)
        for axis in range(3):
            impulse[axis, spot] = got[axis * CELLS : (axis + 1) * CELLS]
    for s, (face, corner, at) in enumerate(((ylow, clow, CELLS - 1), (yhigh, chigh, 0))):
        tiles = [face[SLABS].astype(f32)]
        for n in range(2):
            tiles.append(
                jnp.concatenate(
                    [corner[SLABS + 2 * n + half].astype(f32) for half in range(2)], axis=0
                )
            )
        found = [group(tile, 4) for tile in tiles]
        spots = []
        for (mx, my, _, _), shift in zip(found, (0, 8, CELLS)):
            spot = mx + shift
            keep = my == at
            if shift == 8:
                keep = keep & (mx == CELLS - 1)
            elif shift == CELLS:
                keep = keep & (mx == 0)
            spots.append(jnp.where(keep, spot, -1.0))
        weight = hot(jnp.concatenate(spots, axis=1), FRAME)
        mz = jnp.concatenate([g[2] for g in found], axis=1)
        riser = jnp.concatenate([g[3] for g in found], axis=1)
        at_z, force = force_of(rim[3 * s : 3 * s + 3], weight, mz, riser)
        got = spread(weight, at_z, force)
        for axis in range(3):
            lines[s, axis] = got[axis * FRAME : (axis + 1) * FRAME]

    @pl.loop(0, 18)
    def _(j):
        at = pl.ds(lax.rem(j + 23, FRAME), 1)
        for axis in range(3):
            value = impulse[axis, j]
            before = jnp.where(row == 0, lines[0, axis, at, :], spin(value, 1, 0))
            after = jnp.where(row == CELLS - 1, lines[1, axis, at, :], spin(value, -1, 0))
            tall[axis, j] = 0.5 * value + 0.25 * (before + after)

    @pl.loop(0, CELLS)
    def _(x):
        density = dens[0, x]
        own = []
        speed = []
        for axis in range(3):
            value = 0.5 * tall[axis, x + 1] + 0.25 * (tall[axis, x] + tall[axis, x + 2])
            field[axis, x] = value
            own.append(value)
            speed.append((dens[1 + axis, x] + 0.5 * value) / density)
        square = speed[0] * speed[0] + speed[1] * speed[1] + speed[2] * speed[2]
        work = speed[0] * own[0] + speed[1] * own[1] + speed[2] * own[2]
        at = pl.ds(pl.multiple_of(x * CELLS, CELLS), CELLS)
        for index in range(19):
            value = nxt[index, at, :]
            if index:
                proj_u = along(speed, VELOCITY[index])
                proj_f = along(own, VELOCITY[index])
                bracket = 1.0 + 3.0 * proj_u + 4.5 * proj_u * proj_u - 1.5 * square
                pull = 3.0 * (proj_f - work) + 9.0 * proj_u * proj_f
            else:
                bracket = 1.0 - 1.5 * square
                pull = -3.0 * work
            equil = WEIGHT[index] * density * bracket
            source = (1.0 - 0.5 / RELAX) * WEIGHT[index] * pull
            nxt[index, at, :] = value - (value - equil) / RELAX + source


def on_device(populations, panels, modal_vel, marker_x, marker_y, marker_z, marker_riser):
    f32, bf16 = jnp.float32, jnp.bfloat16
    shape = jax.ShapeDtypeStruct
    devices = lax.axis_size("gx") * lax.axis_size("gy")
    cells = populations.reshape(19, CELLS * CELLS, DEPTH)
    marks = [m.reshape(1, MARKS) for m in (marker_x, marker_y, marker_z, marker_riser)]
    panel = panels.reshape(RISERS, -1)
    modes = panel.shape[1]
    vmem = pl.BlockSpec(memory_space=pltpu.VMEM)
    face = shape((SLABS + 1, CELLS, DEPTH), bf16)
    corner = shape((SLABS + 4, 8, DEPTH), bf16)

    def limit(mib):
        return pltpu.CompilerParams(vmem_limit_bytes=mib << 20)

    xup, xdown, yup, ydown, rows = pl.pallas_call(
        pack_faces,
        out_shape=(face, face, face, face, shape((devices, 128), f32)),
        in_specs=[pl.BlockSpec(memory_space=pl.ANY)] * 7,
        out_specs=(vmem,) * 5,
        scratch_shapes=[
            pltpu.VMEM(cells.shape, f32),
            *[pltpu.VMEM((1, MARKS), jnp.int32)] * 4,
            pltpu.VMEM(panel.shape, bf16),
            pltpu.VMEM(modal_vel.shape, bf16),
            pltpu.VMEM((16, DEPTH), f32),
            pltpu.VMEM((2 * RISERS, modes), f32),
            pltpu.SemaphoreType.DMA((7,)),
        ],
        name="pack_faces",
    )(cells, *marks, panel, modal_vel)

    def ring(axis, toward):
        size = lax.axis_size(axis)
        return [(i, (i + toward) % size) for i in range(size)]

    xlow = lax.ppermute(xup, "gx", ring("gx", 1))
    xhigh = lax.ppermute(xdown, "gx", ring("gx", -1))
    ylow = lax.ppermute(yup, "gy", ring("gy", 1))
    yhigh = lax.ppermute(ydown, "gy", ring("gy", -1))
    table = lax.all_to_all(rows, ("gx", "gy"), 0, 0, tiled=True)
    cup, cdown = pl.pallas_call(
        pack_corners,
        out_shape=(corner, corner),
        in_specs=[vmem] * 2,
        out_specs=(vmem,) * 2,
        scratch_shapes=[pltpu.VMEM((SLABS + 1, CELLS, DEPTH), f32)] * 2,
        compiler_params=limit(8),
        name="pack_corners",
    )(xlow, xhigh)
    clow = lax.ppermute(cup, "gy", ring("gy", 1))
    chigh = lax.ppermute(cdown, "gy", ring("gy", -1))
    nxt, push, field = pl.pallas_call(
        step_kernel,
        out_shape=(
            shape((19, CELLS * CELLS, DEPTH), f32),
            shape((3, 1, MARKS), f32),
            shape((3, CELLS, CELLS, DEPTH), f32),
        ),
        in_specs=[pl.BlockSpec(memory_space=pl.ANY)] + [vmem] * 11,
        out_specs=(vmem,) * 3,
        scratch_shapes=[
            pltpu.VMEM((19, FRAME * CELLS, DEPTH), f32),
            pltpu.VMEM((2, 5, FRAME, DEPTH), f32),
            pltpu.VMEM((2, 2, 3, FRAME, DEPTH), f32),
            pltpu.VMEM((2, 3, FRAME, DEPTH), f32),
            pltpu.VMEM((3, 20, CELLS, DEPTH), f32),
            pltpu.VMEM((3, 20, CELLS, DEPTH), f32),
            pltpu.VMEM((3, 18, CELLS, DEPTH), f32),
            pltpu.VMEM((4, CELLS, CELLS, DEPTH), f32),
            pltpu.VMEM((3, 18, CELLS, DEPTH), f32),
            pltpu.SemaphoreType.DMA,
        ],
        compiler_params=limit(32),
        name="step_kernel",
    )(cells, xlow, xhigh, ylow, yhigh, clow, chigh, *marks, table)
    return (
        nxt.reshape(19, CELLS, CELLS, DEPTH),
        push.transpose(1, 0, 2)[None],
        field,
    )


def solution(mesh):
    in_specs = (
        P(None, "gx", "gy", None),
        P(None, None, ("gx", "gy")),
        P(),
        P("gx", "gy", None),
        P("gx", "gy", None),
        P("gx", "gy", None),
        P("gx", "gy", None),
    )
    out_specs = (P(None, "gx", "gy", None), P("gx", "gy", None, None), P(None, "gx", "gy", None))
    return jax.shard_map(on_device, mesh=mesh, in_specs=in_specs, out_specs=out_specs, check_vma=False)
```

profile of v0, /device:TPU:1, one launch (start us, length us, event | category | flops | bytes accessed | tf_op | source)
XLA Modules:
  0.0 44.8 jit_solution(8799173008853935140)
XLA Ops:
  0.6 0.0 copy-start.4
  0.6 0.0 copy-start.3
  0.7 0.0 copy-start.2
  0.7 0.0 copy-start.1
  0.7 0.0 copy-start
  0.7 3.0 %pack_faces.1 = (bf16[39,16,128]{2,1,0:T(8,128)(2,1)}, bf16[39,16,128]{2,1,0:T(8,128)(2,1)}, bf16[39,16,128]{2,1,0:T(8,128)(2,1)}, bf16[39,16,128]{2,1,0:T(8,128)(2,1)}, f32[128,128]{1,0:T(8,128)}) custom-call(f32[19,256,128]{2,1,0:T(8,128)} %bitcast.14, s32[1,512]{1,0:T(1,128)} %bitcast.17, s32[1,512]{1,0:T(1,128)} %bitcast.19, s32[1,512]{1,0:T(1,128)} %bitcast.21, ...), custom_call_target="tpu_custom_call" | custom-call | tf_op jit(solution)/shard_map/pack_faces/pallas_call | solution.py:457
  3.7 3.1 %collective-permute-start = (bf16[39,16,128]{2,1,0:T(8,128)(2,1)}, bf16[39,16,128]{2,1,0:T(8,128)(2,1)S(1)}, u32[]{:S(2)}, u32[]{:S(2)}) collective-permute-start(bf16[39,16,128]{2,1,0:T(8,128)(2,1)} %get-tuple-element.13), channel_id=1, source_target_pairs={{0,8},{8,16},{16,24},{24,32},{32,40},{40,48},{48,56},{56,64},{64,7... | collective-permute-start | bytes 479240 | tf_op jit(solution)/shard_map/ppermute | solution.py:478
  6.8 0.0 collective-permute-start.1
  6.8 1.3 %collective-permute-start.2 = (bf16[39,16,128]{2,1,0:T(8,128)(2,1)}, bf16[39,16,128]{2,1,0:T(8,128)(2,1)S(1)}, u32[]{:S(2)}, u32[]{:S(2)}) collective-permute-start(bf16[39,16,128]{2,1,0:T(8,128)(2,1)} %get-tuple-element.15), channel_id=1, source_target_pairs={{0,1},{1,2},{2,3},{3,4},{4,5},{5,6},{6,7},{7,0},{8,9},{9,10},{10,1... | collective-permute-start | bytes 479240 | tf_op jit(solution)/shard_map/ppermute | solution.py:480
  8.1 2.4 %collective-permute-start.3 = (bf16[39,16,128]{2,1,0:T(8,128)(2,1)}, bf16[39,16,128]{2,1,0:T(8,128)(2,1)S(1)}, u32[]{:S(2)}, u32[]{:S(2)}) collective-permute-start(bf16[39,16,128]{2,1,0:T(8,128)(2,1)} %get-tuple-element.16), channel_id=1, source_target_pairs={{0,7},{1,0},{2,1},{3,2},{4,3},{5,4},{6,5},{7,6},{8,15},{9,8},{10,9... | collective-permute-start | bytes 479240 | tf_op jit(solution)/shard_map/ppermute | solution.py:481
  10.5 0.0 collective-permute-done.xlow
  10.5 1.5 %collective-permute-done.1.xhigh = bf16[39,16,128]{2,1,0:T(8,128)(2,1)S(1)} collective-permute-done((bf16[39,16,128]{2,1,0:T(8,128)(2,1)}, bf16[39,16,128]{2,1,0:T(8,128)(2,1)S(1)}, u32[]{:S(2)}, u32[]{:S(2)}) %collective-permute-start.1) | collective-permute-done | bytes 159776 | tf_op jit(solution)/shard_map/ppermute | solution.py:479
  12.0 0.1 pack_corners.1
  12.1 1.4 %collective-permute-start.4 = (bf16[42,8,128]{2,1,0:T(8,128)(2,1)S(1)}, bf16[42,8,128]{2,1,0:T(8,128)(2,1)S(1)}, u32[]{:S(2)}, u32[]{:S(2)}) collective-permute-start(bf16[42,8,128]{2,1,0:T(8,128)(2,1)S(1)} %get-tuple-element.17), channel_id=1, source_target_pairs={{0,1},{1,2},{2,3},{3,4},{4,5},{5,6},{6,7},{7,0},{8,9},{9,10},{10,1... | collective-permute-start | bytes 258056 | tf_op jit(solution)/shard_map/ppermute | solution.py:492
  13.5 2.4 %collective-permute-start.5 = (bf16[42,8,128]{2,1,0:T(8,128)(2,1)S(1)}, bf16[42,8,128]{2,1,0:T(8,128)(2,1)S(1)}, u32[]{:S(2)}, u32[]{:S(2)}) collective-permute-start(bf16[42,8,128]{2,1,0:T(8,128)(2,1)S(1)} %get-tuple-element.18), channel_id=1, source_target_pairs={{0,7},{1,0},{2,1},{3,2},{4,3},{5,4},{6,5},{7,6},{8,15},{9,8},{10,9... | collective-permute-start | bytes 258056 | tf_op jit(solution)/shard_map/ppermute | solution.py:493
  16.0 19.4 %all_to_all.11 = f32[128,1,128]{2,1,0:T(1,128)S(1)} all-to-all(f32[128,1,128]{2,1,0:T(1,128)} %bitcast.25), channel_id=1, replica_groups=mesh['gx'=16,'gy'=8] {'gx','gy'}, dimensions={0} | all-to-all | bytes 131072 | tf_op jit(solution)/shard_map/all_to_all | solution.py:482
  35.3 0.0 collective-permute-done.2.ylow
  35.3 0.0 collective-permute-done.3.yhigh
  35.4 0.0 collective-permute-done.4.clow
  35.4 0.0 collective-permute-done.5.chigh
  35.4 0.0 copy-done.4
  35.4 0.0 copy-done.3
  35.4 0.0 copy-done.2
  35.4 0.0 copy-done.1
  35.4 0.0 copy-done
  35.4 9.4 %step_kernel.1 = (f32[19,256,128]{2,1,0:T(8,128)}, f32[3,1,512]{2,1,0:T(1,128)}, f32[3,16,16,128]{3,2,1,0:T(8,128)}) custom-call(f32[19,256,128]{2,1,0:T(8,128)S(1)} %bitcast.15, bf16[39,16,128]{2,1,0:T(8,128)(2,1)S(1)} %collective-permute-done.xlow, bf16[39,16,128]{2,1,0:T(8,128)(2,1)S(1)} %collective-permute-done.1.xhigh, ...), custom_call_target="tpu_custom_call" | custom-call | tf_op jit(solution)/shard_map/step_kernel/pallas_call | solution.py:494
Async XLA Ops:
  0.6 34.7 %copy-start.4 = (s32[1,1,512]{2,1,0:T(1,128)S(1)}, s32[1,1,512]{2,1,0:T(1,128)}, u32[]{:S(2)}) copy-start(s32[1,1,512]{2,1,0:T(1,128)} %param.13) | copy-start | bytes 6148
  0.6 34.7 %copy-start.3 = (s32[1,1,512]{2,1,0:T(1,128)S(1)}, s32[1,1,512]{2,1,0:T(1,128)}, u32[]{:S(2)}) copy-start(s32[1,1,512]{2,1,0:T(1,128)} %param.12) | copy-start | bytes 6148
  0.7 34.7 %copy-start.2 = (s32[1,1,512]{2,1,0:T(1,128)S(1)}, s32[1,1,512]{2,1,0:T(1,128)}, u32[]{:S(2)}) copy-start(s32[1,1,512]{2,1,0:T(1,128)} %param.11) | copy-start | bytes 6148
  0.7 34.7 %copy-start.1 = (s32[1,1,512]{2,1,0:T(1,128)S(1)}, s32[1,1,512]{2,1,0:T(1,128)}, u32[]{:S(2)}) copy-start(s32[1,1,512]{2,1,0:T(1,128)} %param.10) | copy-start | bytes 6148
  0.7 34.7 %copy-start = (f32[19,16,16,128]{3,2,1,0:T(8,128)S(1)}, f32[19,16,16,128]{3,2,1,0:T(8,128)}, u32[]{:S(2)}) copy-start(f32[19,16,16,128]{3,2,1,0:T(8,128)} %param.7) | copy-start | bytes 7471108
  3.7 6.8 %collective-permute-start = (bf16[39,16,128]{2,1,0:T(8,128)(2,1)}, bf16[39,16,128]{2,1,0:T(8,128)(2,1)S(1)}, u32[]{:S(2)}, u32[]{:S(2)}) collective-permute-start(bf16[39,16,128]{2,1,0:T(8,128)(2,1)} %get-tuple-element.13), channel_id=1, source_target_pairs={{0,8},{8,16},{16,24},{24,32},{32,40},{40,48},{48,56},{56,64},{64,7... | collective-permute-start | bytes 479240 | tf_op jit(solution)/shard_map/ppermute | solution.py:478
  6.8 5.2 %collective-permute-start.1 = (bf16[39,16,128]{2,1,0:T(8,128)(2,1)}, bf16[39,16,128]{2,1,0:T(8,128)(2,1)S(1)}, u32[]{:S(2)}, u32[]{:S(2)}) collective-permute-start(bf16[39,16,128]{2,1,0:T(8,128)(2,1)} %get-tuple-element.14), channel_id=1, source_target_pairs={{0,120},{8,0},{16,8},{24,16},{32,24},{40,32},{48,40},{56,48},{64,5... | collective-permute-start | bytes 479240 | tf_op jit(solution)/shard_map/ppermute | solution.py:479
  6.8 28.5 %collective-permute-start.2 = (bf16[39,16,128]{2,1,0:T(8,128)(2,1)}, bf16[39,16,128]{2,1,0:T(8,128)(2,1)S(1)}, u32[]{:S(2)}, u32[]{:S(2)}) collective-permute-start(bf16[39,16,128]{2,1,0:T(8,128)(2,1)} %get-tuple-element.15), channel_id=1, source_target_pairs={{0,1},{1,2},{2,3},{3,4},{4,5},{5,6},{6,7},{7,0},{8,9},{9,10},{10,1... | collective-permute-start | bytes 479240 | tf_op jit(solution)/shard_map/ppermute | solution.py:480
  8.1 27.2 %collective-permute-start.3 = (bf16[39,16,128]{2,1,0:T(8,128)(2,1)}, bf16[39,16,128]{2,1,0:T(8,128)(2,1)S(1)}, u32[]{:S(2)}, u32[]{:S(2)}) collective-permute-start(bf16[39,16,128]{2,1,0:T(8,128)(2,1)} %get-tuple-element.16), channel_id=1, source_target_pairs={{0,7},{1,0},{2,1},{3,2},{4,3},{5,4},{6,5},{7,6},{8,15},{9,8},{10,9... | collective-permute-start | bytes 479240 | tf_op jit(solution)/shard_map/ppermute | solution.py:481
  12.1 23.2 %collective-permute-start.4 = (bf16[42,8,128]{2,1,0:T(8,128)(2,1)S(1)}, bf16[42,8,128]{2,1,0:T(8,128)(2,1)S(1)}, u32[]{:S(2)}, u32[]{:S(2)}) collective-permute-start(bf16[42,8,128]{2,1,0:T(8,128)(2,1)S(1)} %get-tuple-element.17), channel_id=1, source_target_pairs={{0,1},{1,2},{2,3},{3,4},{4,5},{5,6},{6,7},{7,0},{8,9},{9,10},{10,1... | collective-permute-start | bytes 258056 | tf_op jit(solution)/shard_map/ppermute | solution.py:492
  13.5 21.8 %collective-permute-start.5 = (bf16[42,8,128]{2,1,0:T(8,128)(2,1)S(1)}, bf16[42,8,128]{2,1,0:T(8,128)(2,1)S(1)}, u32[]{:S(2)}, u32[]{:S(2)}) collective-permute-start(bf16[42,8,128]{2,1,0:T(8,128)(2,1)S(1)} %get-tuple-element.18), channel_id=1, source_target_pairs={{0,7},{1,0},{2,1},{3,2},{4,3},{5,4},{6,5},{7,6},{8,15},{9,8},{10,9... | collective-permute-start | bytes 258056 | tf_op jit(solution)/shard_map/ppermute | solution.py:493
where the time goes:
time: 44.9 us; the launch traced here: 44.8 us
  blocking collectives  19.4 us (43%)
  Pallas kernels  12.5 us (28%)
  starting transfers between devices  10.6 us (24%)
  waiting for transfers between devices  1.55 us (3%)
  between operations  0.74 us (2%)
    all_to_all x1, blocking collectives, on_device(): table = lax.all_to_all(rows, ('gx', 'gy'), 0, 0, tiled=True)  19.4 us
    pallas_call x1, Pallas kernels, on_device(): pl.pallas_call(step_kernel, out_shape=(shape((19, CELLS * CELLS, DEPTH),...  9.37 us
    ppermute x1, starting transfers between devices, on_device(): xlow = lax.ppermute(xup, 'gx', ring('gx', 1))  3.08 us
    pallas_call x1, Pallas kernels, on_device(): pl.pallas_call(pack_faces, out_shape=(face, face, face, face, shape((devi...  3.03 us
    ppermute x1, starting transfers between devices, on_device(): chigh = lax.ppermute(cdown, 'gy', ring('gy', -1))  2.45 us
    ppermute x1, starting transfers between devices, on_device(): yhigh = lax.ppermute(ydown, 'gy', ring('gy', -1))  2.37 us
    ppermute x1, waiting for transfers between devices, on_device(): xhigh = lax.ppermute(xdown, 'gx', ring('gx', -1))  1.53 us
    ppermute x1, starting transfers between devices, on_device(): clow = lax.ppermute(cup, 'gy', ring('gy', 1))  1.37 us
  transfers between devices with their start and end apart: 6, of which 1 were waited for; matrix products, arithmetic and copies ran while one was open for 0% of the time, Pallas kernels for 0%

commit v1 on v0

v1 whole, which is shorter than its diff:
```python
import jax
import jax.numpy as jnp
from jax import lax
from jax.experimental import pallas as pl
from jax.experimental.pallas import tpu as pltpu
from jax.sharding import PartitionSpec as P

VELOCITY = (
    (0, 0, 0),
    (1, 0, 0),
    (-1, 0, 0),
    (0, 1, 0),
    (0, -1, 0),
    (0, 0, 1),
    (0, 0, -1),
    (1, 1, 0),
    (-1, -1, 0),
    (1, -1, 0),
    (-1, 1, 0),
    (1, 0, 1),
    (-1, 0, -1),
    (1, 0, -1),
    (-1, 0, 1),
    (0, 1, 1),
    (0, -1, -1),
    (0, 1, -1),
    (0, -1, 1),
)
WEIGHT = (1.0 / 3.0,) + (1.0 / 18.0,) * 6 + (1.0 / 36.0,) * 12
RELAX = 0.8
CELLS = 16
DEPTH = 128
MARKS = 512
RISERS = 64
FRAME = 24


def slabs(axis, toward):
    order = []
    for layer in (1, 2, 3):
        for index in range(19):
            if VELOCITY[index][axis] * toward >= layer - 2:
                order.append((layer, index))
    return order


ORDER = {(axis, toward): slabs(axis, toward) for axis in (0, 1) for toward in (1, -1)}
PLACE = {key: {slab: k for k, slab in enumerate(order)} for key, order in ORDER.items()}
SLABS = len(ORDER[0, 1])
INWARD = {toward: [i for i in range(19) if VELOCITY[i][1] == toward] for toward in (1, -1)}


def near(layer, toward):
    return CELLS - layer if toward == 1 else layer - 1


def encode(value, index):
    return (value - WEIGHT[index]).astype(jnp.bfloat16)


def decode(value, index):
    return value.astype(jnp.float32) + WEIGHT[index]


def split(value):
    high = value.astype(jnp.bfloat16)
    low = (value - high.astype(jnp.float32)).astype(jnp.bfloat16)
    return high, low


def pack_x(
    cells_far, mx_far, my_far, mz_far, riser_far, panel_far, modal_far,
    xup, xdown, rows,
    first, last, mx, my, mz, riser, panel, modal, marks, pairs, sems,
):
    span = 3 * CELLS
    copies = [
        pltpu.make_async_copy(far, here, sems.at[n])
        for n, (far, here) in enumerate(
            (
                (modal_far, modal),
                (panel_far, panel),
                (mx_far, mx),
                (my_far, my),
                (mz_far, mz),
                (riser_far, riser),
                (cells_far.at[:, pl.ds(0, span), :], first),
                (cells_far.at[:, pl.ds(CELLS * CELLS - span, span), :], last),
            )
        )
    ]
    for copy in copies:
        copy.start()
    for copy in copies[:6]:
        copy.wait()
    fill_marks(marks, (mx, my, mz, riser))
    for n in range(RISERS):
        both = modal[n].astype(jnp.float32)
        for d in range(2):
            pairs[d * RISERS + n : d * RISERS + n + 1, :] = both[d : d + 1]
    product = lax.dot_general(
        panel[...],
        pairs[...].astype(jnp.bfloat16),
        (((1,), (1,)), ((), ())),
        preferred_element_type=jnp.float32,
    )
    mine = lax.broadcasted_iota(jnp.int32, product.shape, 0) == (
        lax.broadcasted_iota(jnp.int32, product.shape, 1) & (RISERS - 1)
    )
    row = jnp.sum(jnp.where(mine, product, 0.0), axis=0, keepdims=True)
    rows[...] = jnp.broadcast_to(row, rows.shape)
    for copy in copies[6:]:
        copy.wait()
    for out, toward in ((xup, 1), (xdown, -1)):
        for k, (layer, index) in enumerate(ORDER[0, toward]):
            if toward == 1:
                value = last[index, (3 - layer) * CELLS : (4 - layer) * CELLS, :]
            else:
                value = first[index, (layer - 1) * CELLS : layer * CELLS, :]
            out[k] = encode(value, index)
        out[SLABS] = marks[...].astype(jnp.bfloat16)


def fill_marks(marks, sources):
    for attr, source in enumerate(sources):
        for n in range(4):
            marks[attr * 4 + n : attr * 4 + n + 1, :] = source[:, n * 128 : (n + 1) * 128].astype(
                jnp.float32
            )


def pack_y(cells, xlow, xhigh, mx, my, mz, riser, yup, ydown, low, high, marks):
    low[...] = xlow[...].astype(jnp.float32)
    high[...] = xhigh[...].astype(jnp.float32)
    fill_marks(marks, (mx, my, mz, riser))
    place = lax.broadcasted_iota(jnp.int32, (8, DEPTH), 0)
    none = jnp.zeros((8, DEPTH), jnp.float32)
    for out, toward in ((yup, 1), (ydown, -1)):
        for k, (layer, index) in enumerate(ORDER[1, toward]):
            row = near(layer, toward)
            tile = none
            for depth in (1, 2, 3):
                for source, side, at in ((high, -1, depth - 1), (low, 1, 8 - depth)):
                    slot = PLACE[0, side].get((depth, index))
                    if slot is not None:
                        tile = jnp.where(place == at, source[slot, row : row + 1, :], tile)
            own = cells[index, pl.ds(row, CELLS, stride=CELLS), :] - WEIGHT[index]
            out[k] = jnp.concatenate([own, tile], axis=0).astype(jnp.bfloat16)
        for n, source in enumerate((marks[...], low[SLABS], high[SLABS])):
            out[SLABS + n] = jnp.concatenate([source, none], axis=0).astype(jnp.bfloat16)


def moments(reads):
    density = None
    momentum = [None, None, None]
    for index, value in enumerate(reads):
        density = value if density is None else density + value
        for axis in range(3):
            sign = VELOCITY[index][axis]
            if sign == 1:
                momentum[axis] = value if momentum[axis] is None else momentum[axis] + value
            elif sign == -1:
                momentum[axis] = -value if momentum[axis] is None else momentum[axis] - value
    return density, momentum


def along(vector, direction):
    total = None
    for axis in range(3):
        if direction[axis] == 1:
            total = vector[axis] if total is None else total + vector[axis]
        elif direction[axis] == -1:
            total = -vector[axis] if total is None else total - vector[axis]
    return total


def spin(value, shift, axis):
    return pltpu.roll(value, shift % value.shape[axis], axis) if shift else value


def step_kernel(
    cells, xlow, xhigh, ylow, yhigh, own_x, own_y, own_z, own_riser, table,
    nxt_far, push, field_far,
    nxt, field, side, edge, strip, lines, vel, tall, smooth, dens, impulse, sems,
):
    f32, bf16 = jnp.float32, jnp.bfloat16

    def rows_of(column):
        return slice(column * CELLS, (column + 1) * CELLS)

    for message, toward in ((xlow, 1), (xhigh, -1)):
        for k, (layer, index) in enumerate(ORDER[0, toward]):
            column = 8 - layer if toward == 1 else layer - 1
            side[index, rows_of(column), :] = decode(message[k], index)

    for s, (toward, message) in enumerate(((1, ylow), (-1, yhigh))):
        first = 0 if toward == 1 else CELLS - 1
        for n, index in enumerate(INWARD[toward]):
            edge[s, n] = decode(message[PLACE[1, toward][1, index]], index)
        for layer in (1, 2):

            def reads():
                for index in range(19):
                    cx, cy, cz = VELOCITY[index]
                    source = layer + toward * cy
                    if source == 0:
                        value = jnp.concatenate(
                            [
                                cells[index, pl.ds(first, CELLS, stride=CELLS), :],
                                side[index, pl.ds(first, 8, stride=CELLS), :],
                            ],
                            axis=0,
                        )
                    elif source == 1 and cy == toward:
                        value = edge[s, INWARD[toward].index(index)]
                    else:
                        value = decode(message[PLACE[1, toward][source, index]], index)
                    yield spin(spin(value, cx, 0), cz, 1)

            density, momentum = moments(reads())
            for axis in range(3):
                strip[s, layer - 1, axis] = momentum[axis] / density

    row = lax.broadcasted_iota(jnp.int32, (CELLS, DEPTH), 0)

    def column(x, known, keep):
        def reads():
            for index in range(19):
                cx, cy, cz = VELOCITY[index]
                if known:
                    at = (x - cx) % FRAME
                    if at < CELLS:
                        value = cells[index, rows_of(at), :]
                    else:
                        value = side[index, rows_of(at - CELLS), :]
                else:
                    at = x - cx
                    value = cells[index, pl.ds(pl.multiple_of(at * CELLS, CELLS), CELLS), :]
                if cy:
                    s = 0 if cy == 1 else 1
                    line = edge[s, INWARD[cy].index(index), pl.ds(at, 1), :]
                    value = jnp.where(row == (0 if cy == 1 else CELLS - 1), line, spin(value, cy, 0))
                value = spin(value, cz, 1)
                if keep:
                    if known:
                        nxt[index, rows_of(x), :] = value
                    else:
                        nxt[index, pl.ds(pl.multiple_of(x * CELLS, CELLS), CELLS), :] = value
                yield value

        density, momentum = moments(reads())
        at = pl.ds(x % FRAME if known else x, 1)
        if keep:
            dens[0, x] = density
        for axis in range(3):
            speed = momentum[axis] / density
            if keep:
                dens[1 + axis, x] = momentum[axis]
            vel[axis, x + 2] = speed
            lines[0, axis, at, :] = speed[0:1]
            lines[1, axis, at, :] = speed[CELLS - 1 : CELLS]

    for x in (-2, -1, 0, CELLS - 1, CELLS, CELLS + 1):
        column(x, True, 0 <= x < CELLS)

    @pl.loop(1, CELLS - 1)
    def _(x):
        column(x, False, True)

    @pl.loop(0, 20, unroll=4)
    def _(j):
        at = pl.ds(lax.rem(j + 22, FRAME), 1)
        for axis in range(3):
            value = vel[axis, j]
            before = jnp.where(row == 0, strip[0, 0, axis, at, :], spin(value, 1, 0))
            after = jnp.where(row == CELLS - 1, strip[1, 0, axis, at, :], spin(value, -1, 0))
            tall[axis, j] = 0.5 * value + 0.25 * (before + after)

    @pl.loop(0, 18, unroll=3)
    def _(j):
        for axis in range(3):
            value = 0.5 * tall[axis, j + 1] + 0.25 * (tall[axis, j] + tall[axis, j + 2])
            high, low = split(value)
            smooth[axis, j, :, :DEPTH] = high
            smooth[axis, j, :, DEPTH:] = low

    place = lax.broadcasted_iota(jnp.int32, (FRAME, DEPTH), 0)
    inside = (place <= CELLS) | (place == FRAME - 1)
    rim = [[], []]
    for s in range(2):
        for axis in range(3):
            value = 0.5 * strip[s, 0, axis] + 0.25 * (strip[s, 1, axis] + lines[s, axis])
            value = 0.5 * value + 0.25 * (spin(value, 1, 0) + spin(value, -1, 0))
            rim[s].append(jnp.where(inside, value, 0.0))

    goal = jnp.concatenate(split(table[...].T), axis=1)
    step = 256

    def hot(position, count):
        shape = (count, position.shape[1])
        return lax.broadcasted_iota(jnp.int32, shape, 0).astype(f32) == position

    def ones(mask):
        return jnp.where(mask, 1.0, 0.0).astype(bf16)

    def force_of(sources, count, spot, z, riser):
        at_z = ones(hot(z, DEPTH))
        picked = jnp.dot(
            sources, jnp.concatenate([at_z, at_z], axis=0), preferred_element_type=f32
        )
        at_riser = hot(riser, RISERS)
        weight = hot(spot, count)
        out = []
        for axis in range(3):
            start = 2 * RISERS + axis * count
            speed = picked[start : start + count]
            value = -jnp.sum(jnp.where(weight, speed, 0.0), axis=0, keepdims=True)
            if axis < 2:
                some = picked[axis * RISERS : (axis + 1) * RISERS]
                value = value + jnp.sum(jnp.where(at_riser, some, 0.0), axis=0, keepdims=True)
            out.append(2.0 * value)
        return at_z, out

    contract = (((1,), (1,)), ((), ()))

    def parts(force):
        found = []
        for value in force:
            high, low = split(value)
            found.append((high.astype(f32), low.astype(f32)))
        return found

    def spread(count, spot, at_z, force):
        weight = hot(spot, count)
        halves = []
        for half in range(2):
            rows = [jnp.where(weight, value[half], 0.0) for value in parts(force)]
            halves.append(jnp.concatenate(rows, axis=0).astype(bf16))
        return lax.dot_general(
            jnp.concatenate(halves, axis=1),
            jnp.concatenate([at_z, at_z], axis=1),
            contract,
            preferred_element_type=f32,
        )

    def take(slab, attr, n):
        at = attr * 4 + 2 * n
        return jnp.concatenate([slab[at : at + 1, :], slab[at + 1 : at + 2, :]], axis=1)

    inner = [smooth[axis, 1 : CELLS + 1].reshape(CELLS * CELLS, 2 * DEPTH) for axis in range(3)]
    sources = jnp.concatenate([goal, *inner], axis=0)
    total = None
    for n in range(MARKS // step):
        here = slice(n * step, (n + 1) * step)
        mx, my, mz, riser = (
            m[:, here].astype(f32) for m in (own_x, own_y, own_z, own_riser)
        )
        spot = mx * CELLS + my
        _, force = force_of(sources, CELLS * CELLS, spot, mz, riser)
        where_z = hot(mz, DEPTH)
        halves = []
        for half in range(2):
            rows = [jnp.where(where_z, value[half], 0.0) for value in parts(force)]
            halves.append(jnp.concatenate(rows, axis=0).astype(bf16))
        at_cell = ones(hot(spot, CELLS * CELLS))
        got = lax.dot_general(
            jnp.concatenate([at_cell, at_cell], axis=1),
            jnp.concatenate(halves, axis=1),
            contract,
            preferred_element_type=f32,
        )
        total = got if total is None else total + got
        for axis in range(3):
            push[axis, :, here] = force[axis]
    for axis in range(3):
        impulse[axis, 1 : CELLS + 1] = total[:, axis * DEPTH : (axis + 1) * DEPTH].reshape(
            CELLS, CELLS, DEPTH
        )
    for message, at, spot_x in ((xlow, CELLS - 1, 0), (xhigh, 0, CELLS + 1)):
        sources = jnp.concatenate([goal, *(smooth[axis, spot_x] for axis in range(3))], axis=0)
        slab = message[SLABS].astype(f32)
        total = None
        for n in range(MARKS // step):
            mx, my, mz, riser = (take(slab, attr, n) for attr in range(4))
            spot = jnp.where(mx == at, my, -1.0)
            at_z, force = force_of(sources, CELLS, spot, mz, riser)
            got = spread(CELLS, spot, at_z, force)
            total = got if total is None else total + got
        for axis in range(3):
            impulse[axis, spot_x] = total[axis * CELLS : (axis + 1) * CELLS]
    for s, (message, at) in enumerate(((ylow, CELLS - 1), (yhigh, 0))):
        halves = [jnp.concatenate(split(value), axis=1) for value in rim[s]]
        sources = jnp.concatenate([goal, *halves], axis=0)
        total = None
        for tile in range(3):
            slab = message[SLABS + tile].astype(f32)
            for n in range(MARKS // step):
                mx, my, mz, riser = (take(slab, attr, n) for attr in range(4))
                keep = my == at
                if tile == 1:
                    keep = keep & (mx == CELLS - 1)
                elif tile == 2:
                    keep = keep & (mx == 0)
                spot = jnp.where(keep, mx + (0, 8, CELLS)[tile], -1.0)
                at_z, force = force_of(sources, FRAME, spot, mz, riser)
                got = spread(FRAME, spot, at_z, force)
                total = got if total is None else total + got
        for axis in range(3):
            lines[s, axis] = total[axis * FRAME : (axis + 1) * FRAME]

    @pl.loop(0, 18, unroll=3)
    def _(j):
        at = pl.ds(lax.rem(j + 23, FRAME), 1)
        for axis in range(3):
            value = impulse[axis, j]
            before = jnp.where(row == 0, lines[0, axis, at, :], spin(value, 1, 0))
            after = jnp.where(row == CELLS - 1, lines[1, axis, at, :], spin(value, -1, 0))
            tall[axis, j] = 0.5 * value + 0.25 * (before + after)

    rate = 1.0 / RELAX
    gain = 1.0 - 0.5 / RELAX

    def collide(x):
        density = dens[0, x]
        own, speed = [], []
        for axis in range(3):
            value = 0.5 * tall[axis, x + 1] + 0.25 * (tall[axis, x] + tall[axis, x + 2])
            field[axis, x] = value
            own.append(value)
            speed.append((dens[1 + axis, x] + 0.5 * value) / density)
        square = speed[0] * speed[0] + speed[1] * speed[1] + speed[2] * speed[2]
        work = speed[0] * own[0] + speed[1] * own[1] + speed[2] * own[2]
        base = rate * density * (1.0 - 1.5 * square) - 3.0 * gain * work
        flow = [density * value for value in speed]
        even = [4.5 * rate * a + 9.0 * gain * b for a, b in zip(flow, own)]
        odd = [3.0 * rate * a + 3.0 * gain * b for a, b in zip(flow, own)]
        at = pl.ds(pl.multiple_of(x * CELLS, CELLS), CELLS)
        nxt[0, at, :] = (1.0 - rate) * nxt[0, at, :] + WEIGHT[0] * base
        for weight, indices in ((WEIGHT[1], (1, 3, 5)), (WEIGHT[7], (7, 9, 11, 13, 15, 17))):
            scaled = weight * base
            wide_even = [weight * value for value in even]
            wide_odd = [weight * value for value in odd]
            for index in indices:
                direction = VELOCITY[index]
                both = scaled + along(speed, direction) * along(wide_even, direction)
                apart = along(wide_odd, direction)
                nxt[index, at, :] = (1.0 - rate) * nxt[index, at, :] + (both + apart)
                nxt[index + 1, at, :] = (1.0 - rate) * nxt[index + 1, at, :] + (both - apart)

    copies = []
    chunk = 4
    for n in range(CELLS // chunk):

        @pl.loop(n * chunk, (n + 1) * chunk)
        def _(x):
            collide(x)

        cells_at = pl.ds(n * chunk * CELLS, chunk * CELLS)
        copies.append(
            pltpu.make_async_copy(nxt.at[:, cells_at, :], nxt_far.at[:, cells_at, :], sems.at[2 * n])
        )
        at = pl.ds(n * chunk, chunk)
        copies.append(pltpu.make_async_copy(field.at[:, at], field_far.at[:, at], sems.at[2 * n + 1]))
        for copy in copies[-2:]:
            copy.start()
    for copy in copies:
        copy.wait()


def on_device(populations, panels, modal_vel, marker_x, marker_y, marker_z, marker_riser):
    f32, bf16 = jnp.float32, jnp.bfloat16
    shape = jax.ShapeDtypeStruct
    devices = lax.axis_size("gx") * lax.axis_size("gy")
    cells = populations.reshape(19, CELLS * CELLS, DEPTH)
    marks = [m.reshape(1, MARKS) for m in (marker_x, marker_y, marker_z, marker_riser)]
    panel = panels.reshape(RISERS, -1)
    modes = panel.shape[1]
    vmem = pl.BlockSpec(memory_space=pltpu.VMEM)
    face = shape((SLABS + 1, CELLS, DEPTH), bf16)
    strip = shape((SLABS + 3, FRAME, DEPTH), bf16)

    def limit(mib):
        return pltpu.CompilerParams(vmem_limit_bytes=mib << 20)

    anywhere = pl.BlockSpec(memory_space=pl.ANY)
    xup, xdown, rows = pl.pallas_call(
        pack_x,
        out_shape=(face, face, shape((devices, 128), f32)),
        in_specs=[anywhere] * 7,
        out_specs=(vmem,) * 3,
        scratch_shapes=[
            *[pltpu.VMEM((19, 3 * CELLS, DEPTH), f32)] * 2,
            *[pltpu.VMEM((1, MARKS), jnp.int32)] * 4,
            pltpu.VMEM(panel.shape, bf16),
            pltpu.VMEM(modal_vel.shape, bf16),
            pltpu.VMEM((16, DEPTH), f32),
            pltpu.VMEM((2 * RISERS, modes), f32),
            pltpu.SemaphoreType.DMA((8,)),
        ],
        name="pack_x",
    )(cells, *marks, panel, modal_vel)

    def ring(axis, toward):
        size = lax.axis_size(axis)
        return [(i, (i + toward) % size) for i in range(size)]

    xlow = lax.ppermute(xup, "gx", ring("gx", 1))
    xhigh = lax.ppermute(xdown, "gx", ring("gx", -1))
    table = lax.all_to_all(rows, ("gx", "gy"), 0, 0, tiled=True)
    yup, ydown = pl.pallas_call(
        pack_y,
        out_shape=(strip, strip),
        in_specs=[vmem] * 7,
        out_specs=(vmem,) * 2,
        scratch_shapes=[
            *[pltpu.VMEM((SLABS + 1, CELLS, DEPTH), f32)] * 2,
            pltpu.VMEM((16, DEPTH), f32),
        ],
        compiler_params=limit(8),
        name="pack_y",
    )(cells, xlow, xhigh, *marks)
    ylow = lax.ppermute(yup, "gy", ring("gy", 1))
    yhigh = lax.ppermute(ydown, "gy", ring("gy", -1))
    nxt, push, field = pl.pallas_call(
        step_kernel,
        out_shape=(
            shape((19, CELLS * CELLS, DEPTH), f32),
            shape((3, 1, MARKS), f32),
            shape((3, CELLS, CELLS, DEPTH), f32),
        ),
        in_specs=[vmem] * 10,
        out_specs=(anywhere, vmem, anywhere),
        scratch_shapes=[
            pltpu.VMEM((19, CELLS * CELLS, DEPTH), f32),
            pltpu.VMEM((3, CELLS, CELLS, DEPTH), f32),
            pltpu.VMEM((19, 8 * CELLS, DEPTH), f32),
            pltpu.VMEM((2, 5, FRAME, DEPTH), f32),
            pltpu.VMEM((2, 2, 3, FRAME, DEPTH), f32),
            pltpu.VMEM((2, 3, FRAME, DEPTH), f32),
            pltpu.VMEM((3, 20, CELLS, DEPTH), f32),
            pltpu.VMEM((3, 20, CELLS, DEPTH), f32),
            pltpu.VMEM((3, 18, CELLS, 2 * DEPTH), bf16),
            pltpu.VMEM((4, CELLS, CELLS, DEPTH), f32),
            pltpu.VMEM((3, 18, CELLS, DEPTH), f32),
            pltpu.SemaphoreType.DMA((8,)),
        ],
        compiler_params=limit(32),
        name="step_kernel",
    )(cells, xlow, xhigh, ylow, yhigh, *marks, table)
    return (
        nxt.reshape(19, CELLS, CELLS, DEPTH),
        push.transpose(1, 0, 2)[None],
        field,
    )


def solution(mesh):
    in_specs = (
        P(None, "gx", "gy", None),
        P(None, None, ("gx", "gy")),
        P(),
        P("gx", "gy", None),
        P("gx", "gy", None),
        P("gx", "gy", None),
        P("gx", "gy", None),
    )
    out_specs = (P(None, "gx", "gy", None), P("gx", "gy", None, None), P(None, "gx", "gy", None))
    return jax.shard_map(on_device, mesh=mesh, in_specs=in_specs, out_specs=out_specs, check_vma=False)
```

time: 44.9 us -> 41.2 us (0.918)
  starting transfers between devices: 10.6 us -> 6.9 us
  waiting for transfers between devices: 1.55 us -> 5.21 us
  Pallas kernels: 12.5 us -> 9.77 us
  blocking collectives: 19.4 us -> 18.5 us
    ppermute x2 -> x0, starting transfers between devices: 3.81 us -> none  [the longest x1 2.45 us: on_device(): chigh = lax.ppermute(cdown, 'gy', ring('gy', -1))]
    ppermute x1, waiting for transfers between devices: 0.01 us -> 2.53 us  [on_device(): xlow = lax.ppermute(xup, 'gx', ring('gx', 1))]
    pallas_call x1, Pallas kernels: 9.37 us -> 7.07 us  [on_device(): pl.pallas_call(step_kernel, out_shape=(shape((19, CELLS * CELLS, DEPTH),...]
    ppermute x1, waiting for transfers between devices: 1.53 us -> 2.67 us  [on_device(): xhigh = lax.ppermute(xdown, 'gx', ring('gx', -1))]
    all_to_all x1, blocking collectives: 19.4 us -> 18.5 us  [on_device(): table = lax.all_to_all(rows, ('gx', 'gy'), 0, 0, tiled=True)]
    pallas_call x2, Pallas kernels: 3.16 us -> 2.7 us  [the longest x1 2.28 us: on_device(): pl.pallas_call(pack_x, out_shape=(face, face, shape((devices, 128), f32))...]
  transfers between devices with their start and end apart: 6 -> 4, of which waited for: 1 -> 2; matrix products, arithmetic and copies ran while one was open for 0% -> 0% of each run, Pallas kernels for 0% -> 0%
where the time goes in v1:
time: 41.2 us; the launch traced here: 41.1 us
  blocking collectives  18.5 us (45%)
  Pallas kernels  9.77 us (24%)
  starting transfers between devices  6.9 us (17%)
  waiting for transfers between devices  5.21 us (13%)
  between operations  0.72 us (2%)
    all_to_all x1, blocking collectives, on_device(): table = lax.all_to_all(rows, ('gx', 'gy'), 0, 0, tiled=True)  18.5 us
    pallas_call x1, Pallas kernels, on_device(): pl.pallas_call(step_kernel, out_shape=(shape((19, CELLS * CELLS, DEPTH),...  7.07 us
    ppermute x1, starting transfers between devices, on_device(): xlow = lax.ppermute(xup, 'gx', ring('gx', 1))  3.08 us
    ppermute x1, waiting for transfers between devices, on_device(): xhigh = lax.ppermute(xdown, 'gx', ring('gx', -1))  2.67 us
    ppermute x1, waiting for transfers between devices, on_device(): xlow = lax.ppermute(xup, 'gx', ring('gx', 1))  2.53 us
    ppermute x1, starting transfers between devices, on_device(): yhigh = lax.ppermute(ydown, 'gy', ring('gy', -1))  2.45 us
    pallas_call x1, Pallas kernels, on_device(): pl.pallas_call(pack_x, out_shape=(face, face, shape((devices, 128), f32))...  2.28 us
    ppermute x1, starting transfers between devices, on_device(): ylow = lax.ppermute(yup, 'gy', ring('gy', 1))  1.37 us
  transfers between devices with their start and end apart: 4, of which 2 were waited for; matrix products, arithmetic and copies ran while one was open for 0% of the time, Pallas kernels for 0%

profile of v1, /device:TPU:1, one launch (start us, length us, event | category | flops | bytes accessed | tf_op | source)
XLA Modules:
  0.0 41.1 jit_solution(5830457966183761009)
XLA Ops:
  0.6 0.0 copy-start.4
  0.6 0.0 copy-start.3
  0.7 0.0 copy-start.2
  0.7 0.0 copy-start.1
  0.7 0.0 copy-start
  0.7 2.3 %pack_x.1 = (bf16[39,16,128]{2,1,0:T(8,128)(2,1)}, bf16[39,16,128]{2,1,0:T(8,128)(2,1)}, f32[128,128]{1,0:T(8,128)}) custom-call(f32[19,256,128]{2,1,0:T(8,128)} %bitcast.14, s32[1,512]{1,0:T(1,128)} %bitcast.18, s32[1,512]{1,0:T(1,128)} %bitcast.21, s32[1,512]{1,0:T(1,128)} %bitcast.24, s32[1,512]{1,0:T(1,128)} %bitcast.27, bf16[64,200]{1,0:T(8,128)(2,1)} %bitcast.31, ...), custom_call_target="tpu_custom_call" | custom-call | tf_op jit(solution)/shard_map/pack_x/pallas_call | solution.py:486
  3.0 0.0 copy-start.5
  3.0 3.1 %collective-permute-start = (bf16[39,16,128]{2,1,0:T(8,128)(2,1)}, bf16[39,16,128]{2,1,0:T(8,128)(2,1)S(1)}, u32[]{:S(2)}, u32[]{:S(2)}) collective-permute-start(bf16[39,16,128]{2,1,0:T(8,128)(2,1)} %get-tuple-element.11), channel_id=1, source_target_pairs={{0,8},{8,16},{16,24},{24,32},{32,40},{40,48},{48,56},{56,64},{64,7... | collective-permute-start | bytes 479240 | tf_op jit(solution)/shard_map/ppermute | solution.py:507
  6.1 0.0 collective-permute-start.1
  6.1 2.5 %collective-permute-done.xlow = bf16[39,16,128]{2,1,0:T(8,128)(2,1)S(1)} collective-permute-done((bf16[39,16,128]{2,1,0:T(8,128)(2,1)}, bf16[39,16,128]{2,1,0:T(8,128)(2,1)S(1)}, u32[]{:S(2)}, u32[]{:S(2)}) %collective-permute-start) | collective-permute-done | bytes 159776 | tf_op jit(solution)/shard_map/ppermute | solution.py:507
  8.6 2.7 %collective-permute-done.1.xhigh = bf16[39,16,128]{2,1,0:T(8,128)(2,1)S(1)} collective-permute-done((bf16[39,16,128]{2,1,0:T(8,128)(2,1)}, bf16[39,16,128]{2,1,0:T(8,128)(2,1)S(1)}, u32[]{:S(2)}, u32[]{:S(2)}) %collective-permute-start.1) | collective-permute-done | bytes 159776 | tf_op jit(solution)/shard_map/ppermute | solution.py:508
  11.3 0.0 copy-done.4
  11.3 0.0 copy-done.3
  11.3 0.0 copy-done.2
  11.3 0.0 copy-done.1
  11.3 0.0 copy-done
  11.3 0.4 %pack_y.1 = (bf16[41,24,128]{2,1,0:T(8,128)(2,1)S(1)}, bf16[41,24,128]{2,1,0:T(8,128)(2,1)S(1)}) custom-call(f32[19,256,128]{2,1,0:T(8,128)S(1)} %bitcast.15, bf16[39,16,128]{2,1,0:T(8,128)(2,1)S(1)} %collective-permute-done.xlow, bf16[39,16,128]{2,1,0:T(8,128)(2,1)S(1)} %collective-permute-done.1.xhigh, s32[1,512]{1,0:T(1,128)S(1)} %bitcast.19, ...), custom_call_target="tpu_custom_call" | custom-call | tf_op jit(solution)/shard_map/pack_y/pallas_call | solution.py:510
  11.7 1.4 %collective-permute-start.2 = (bf16[41,24,128]{2,1,0:T(8,128)(2,1)S(1)}, bf16[41,24,128]{2,1,0:T(8,128)(2,1)S(1)}, u32[]{:S(2)}, u32[]{:S(2)}) collective-permute-start(bf16[41,24,128]{2,1,0:T(8,128)(2,1)S(1)} %get-tuple-element.13), channel_id=1, source_target_pairs={{0,1},{1,2},{2,3},{3,4},{4,5},{5,6},{6,7},{7,0},{8,9},{9,10},{10,1... | collective-permute-start | bytes 755720 | tf_op jit(solution)/shard_map/ppermute | solution.py:522
  13.1 2.4 %collective-permute-start.3 = (bf16[41,24,128]{2,1,0:T(8,128)(2,1)S(1)}, bf16[41,24,128]{2,1,0:T(8,128)(2,1)S(1)}, u32[]{:S(2)}, u32[]{:S(2)}) collective-permute-start(bf16[41,24,128]{2,1,0:T(8,128)(2,1)S(1)} %get-tuple-element.14), channel_id=1, source_target_pairs={{0,7},{1,0},{2,1},{3,2},{4,3},{5,4},{6,5},{7,6},{8,15},{9,8},{10,9... | collective-permute-start | bytes 755720 | tf_op jit(solution)/shard_map/ppermute | solution.py:523
  15.5 0.0 copy-done.5
  15.5 18.5 %all_to_all.11 = f32[128,1,128]{2,1,0:T(1,128)S(1)} all-to-all(f32[128,1,128]{2,1,0:T(1,128)S(1)} %bitcast.30), channel_id=1, replica_groups=mesh['gx'=16,'gy'=8] {'gx','gy'}, dimensions={0} | all-to-all | bytes 131072 | tf_op jit(solution)/shard_map/all_to_all | solution.py:509
  34.0 0.0 collective-permute-done.2.ylow
  34.0 0.0 collective-permute-done.3.yhigh
  34.0 7.1 %step_kernel.1 = (f32[19,256,128]{2,1,0:T(8,128)}, f32[3,1,512]{2,1,0:T(1,128)}, f32[3,16,16,128]{3,2,1,0:T(8,128)}) custom-call(f32[19,256,128]{2,1,0:T(8,128)S(1)} %bitcast.16, bf16[39,16,128]{2,1,0:T(8,128)(2,1)S(1)} %collective-permute-done.xlow, bf16[39,16,128]{2,1,0:T(8,128)(2,1)S(1)} %collective-permute-done.1.xhigh, ...), custom_call_target="tpu_custom_call" | custom-call | tf_op jit(solution)/shard_map/step_kernel/pallas_call | solution.py:524
Async XLA Ops:
  0.6 10.6 %copy-start.4 = (s32[1,1,512]{2,1,0:T(1,128)S(1)}, s32[1,1,512]{2,1,0:T(1,128)}, u32[]{:S(2)}) copy-start(s32[1,1,512]{2,1,0:T(1,128)} %param.13) | copy-start | bytes 6148
  0.6 10.6 %copy-start.3 = (s32[1,1,512]{2,1,0:T(1,128)S(1)}, s32[1,1,512]{2,1,0:T(1,128)}, u32[]{:S(2)}) copy-start(s32[1,1,512]{2,1,0:T(1,128)} %param.12) | copy-start | bytes 6148
  0.7 10.6 %copy-start.2 = (s32[1,1,512]{2,1,0:T(1,128)S(1)}, s32[1,1,512]{2,1,0:T(1,128)}, u32[]{:S(2)}) copy-start(s32[1,1,512]{2,1,0:T(1,128)} %param.11) | copy-start | bytes 6148
  0.7 10.6 %copy-start.1 = (s32[1,1,512]{2,1,0:T(1,128)S(1)}, s32[1,1,512]{2,1,0:T(1,128)}, u32[]{:S(2)}) copy-start(s32[1,1,512]{2,1,0:T(1,128)} %param.10) | copy-start | bytes 6148
  0.7 10.6 %copy-start = (f32[19,16,16,128]{3,2,1,0:T(8,128)S(1)}, f32[19,16,16,128]{3,2,1,0:T(8,128)}, u32[]{:S(2)}) copy-start(f32[19,16,16,128]{3,2,1,0:T(8,128)} %param.7) | copy-start | bytes 7471108
  3.0 12.6 %copy-start.5 = (f32[128,128]{1,0:T(8,128)S(1)}, f32[128,128]{1,0:T(8,128)}, u32[]{:S(2)}) copy-start(f32[128,128]{1,0:T(8,128)} %get-tuple-element.15) | copy-start | bytes 196612
  3.0 5.6 %collective-permute-start = (bf16[39,16,128]{2,1,0:T(8,128)(2,1)}, bf16[39,16,128]{2,1,0:T(8,128)(2,1)S(1)}, u32[]{:S(2)}, u32[]{:S(2)}) collective-permute-start(bf16[39,16,128]{2,1,0:T(8,128)(2,1)} %get-tuple-element.11), channel_id=1, source_target_pairs={{0,8},{8,16},{16,24},{24,32},{32,40},{40,48},{48,56},{56,64},{64,7... | collective-permute-start | bytes 479240 | tf_op jit(solution)/shard_map/ppermute | solution.py:507
  6.1 5.2 %collective-permute-start.1 = (bf16[39,16,128]{2,1,0:T(8,128)(2,1)}, bf16[39,16,128]{2,1,0:T(8,128)(2,1)S(1)}, u32[]{:S(2)}, u32[]{:S(2)}) collective-permute-start(bf16[39,16,128]{2,1,0:T(8,128)(2,1)} %get-tuple-element.12), channel_id=1, source_target_pairs={{0,120},{8,0},{16,8},{24,16},{32,24},{40,32},{48,40},{56,48},{64,5... | collective-permute-start | bytes 479240 | tf_op jit(solution)/shard_map/ppermute | solution.py:508
  11.7 22.3 %collective-permute-start.2 = (bf16[41,24,128]{2,1,0:T(8,128)(2,1)S(1)}, bf16[41,24,128]{2,1,0:T(8,128)(2,1)S(1)}, u32[]{:S(2)}, u32[]{:S(2)}) collective-permute-start(bf16[41,24,128]{2,1,0:T(8,128)(2,1)S(1)} %get-tuple-element.13), channel_id=1, source_target_pairs={{0,1},{1,2},{2,3},{3,4},{4,5},{5,6},{6,7},{7,0},{8,9},{9,10},{10,1... | collective-permute-start | bytes 755720 | tf_op jit(solution)/shard_map/ppermute | solution.py:522
  13.1 20.9 %collective-permute-start.3 = (bf16[41,24,128]{2,1,0:T(8,128)(2,1)S(1)}, bf16[41,24,128]{2,1,0:T(8,128)(2,1)S(1)}, u32[]{:S(2)}, u32[]{:S(2)}) collective-permute-start(bf16[41,24,128]{2,1,0:T(8,128)(2,1)S(1)} %get-tuple-element.14), channel_id=1, source_target_pairs={{0,7},{1,0},{2,1},{3,2},{4,3},{5,4},{6,5},{7,6},{8,15},{9,8},{10,9... | collective-permute-start | bytes 755720 | tf_op jit(solution)/shard_map/ppermute | solution.py:523

commit v2 on v1

--- a/solution.py
+++ b/solution.py
@@ -47,6 +47,9 @@
 ORDER = {(axis, toward): slabs(axis, toward) for axis in (0, 1) for toward in (1, -1)}
 PLACE = {key: {slab: k for k, slab in enumerate(order)} for key, order in ORDER.items()}
 SLABS = len(ORDER[0, 1])
+INTO = 5
+SUMS = 7
+YSLABS = INTO + 2 * SUMS
 INWARD = {toward: [i for i in range(19) if VELOCITY[i][1] == toward] for toward in (1, -1)}
 
 
@@ -135,25 +138,43 @@
     fill_marks(marks, (mx, my, mz, riser))
     place = lax.broadcasted_iota(jnp.int32, (8, DEPTH), 0)
     none = jnp.zeros((8, DEPTH), jnp.float32)
+
+    def frame(layer, index, toward):
+        row = near(layer, toward)
+        tile = none
+        for depth in (1, 2, 3):
+            for source, side, at in ((high, -1, depth - 1), (low, 1, 8 - depth)):
+                slot = PLACE[0, side].get((depth, index))
+                if slot is not None:
+                    tile = jnp.where(place == at, source[slot, row : row + 1, :], tile)
+        own = cells[index, pl.ds(row, CELLS, stride=CELLS), :] - WEIGHT[index]
+        return jnp.concatenate([own, tile], axis=0)
+
     for out, toward in ((yup, 1), (ydown, -1)):
-        for k, (layer, index) in enumerate(ORDER[1, toward]):
-            row = near(layer, toward)
-            tile = none
-            for depth in (1, 2, 3):
-                for source, side, at in ((high, -1, depth - 1), (low, 1, 8 - depth)):
-                    slot = PLACE[0, side].get((depth, index))
-                    if slot is not None:
-                        tile = jnp.where(place == at, source[slot, row : row + 1, :], tile)
-            own = cells[index, pl.ds(row, CELLS, stride=CELLS), :] - WEIGHT[index]
-            out[k] = jnp.concatenate([own, tile], axis=0).astype(jnp.bfloat16)
+        for n, index in enumerate(INWARD[toward]):
+            out[n] = frame(1, index, toward).astype(jnp.bfloat16)
+
+        def reads(cell):
+            for index in range(19):
+                cx, cy, cz = VELOCITY[index]
+                layer = cell + toward * cy
+                if layer:
+                    value = frame(layer, index, toward) + WEIGHT[index]
+                    yield index, spin(spin(value, cx, 0), cz, 1)
+
+        density, momentum = moments(reads(2))
+        sums = [value / density for value in momentum]
+        density, momentum = moments(reads(1))
+        for k, value in enumerate([*sums, density, *momentum]):
+            out[INTO + 2 * k], out[INTO + 2 * k + 1] = split(value)
         for n, source in enumerate((marks[...], low[SLABS], high[SLABS])):
-            out[SLABS + n] = jnp.concatenate([source, none], axis=0).astype(jnp.bfloat16)
+            out[YSLABS + n] = jnp.concatenate([source, none], axis=0).astype(jnp.bfloat16)
 
 
 def moments(reads):
     density = None
     momentum = [None, None, None]
-    for index, value in enumerate(reads):
+    for index, value in reads:
         density = value if density is None else density + value
         for axis in range(3):
             sign = VELOCITY[index][axis]
@@ -178,13 +199,7 @@
     return pltpu.roll(value, shift % value.shape[axis], axis) if shift else value
 
 
-def step_kernel(
-    cells, xlow, xhigh, ylow, yhigh, own_x, own_y, own_z, own_riser, table,
-    nxt_far, push, field_far,
-    nxt, field, side, edge, strip, lines, vel, tall, smooth, dens, impulse, sems,
-):
-    f32, bf16 = jnp.float32, jnp.bfloat16
-
+def columns(cells, xlow, xhigh, sums, vel, smooth, share, side, tall):
     def rows_of(column):
         return slice(column * CELLS, (column + 1) * CELLS)
 
@@ -193,37 +208,33 @@
             column = 8 - layer if toward == 1 else layer - 1
             side[index, rows_of(column), :] = decode(message[k], index)
 
-    for s, (toward, message) in enumerate(((1, ylow), (-1, yhigh))):
+    for s, toward in enumerate((1, -1)):
         first = 0 if toward == 1 else CELLS - 1
-        for n, index in enumerate(INWARD[toward]):
-            edge[s, n] = decode(message[PLACE[1, toward][1, index]], index)
-        for layer in (1, 2):
-
-            def reads():
-                for index in range(19):
-                    cx, cy, cz = VELOCITY[index]
-                    source = layer + toward * cy
-                    if source == 0:
-                        value = jnp.concatenate(
-                            [
-                                cells[index, pl.ds(first, CELLS, stride=CELLS), :],
-                                side[index, pl.ds(first, 8, stride=CELLS), :],
-                            ],
-                            axis=0,
-                        )
-                    elif source == 1 and cy == toward:
-                        value = edge[s, INWARD[toward].index(index)]
-                    else:
-                        value = decode(message[PLACE[1, toward][source, index]], index)
-                    yield spin(spin(value, cx, 0), cz, 1)
-
-            density, momentum = moments(reads())
-            for axis in range(3):
-                strip[s, layer - 1, axis] = momentum[axis] / density
+
+        def outward():
+            for index in INWARD[-toward]:
+                cx, _, cz = VELOCITY[index]
+                value = jnp.concatenate(
+                    [
+                        cells[index, pl.ds(first, CELLS, stride=CELLS), :],
+                        side[index, pl.ds(first, 8, stride=CELLS), :],
+                    ],
+                    axis=0,
+                )
+                yield index, spin(spin(value, cx, 0), cz, 1)
+
+        density, momentum = moments(outward())
+        for k, value in enumerate([density, *momentum]):
+            share[s, k] = value
 
     row = lax.broadcasted_iota(jnp.int32, (CELLS, DEPTH), 0)
 
-    def column(x, known, keep):
+    def one(x, known):
+        if known:
+            here = rows_of(x % FRAME)
+        else:
+            here = pl.ds(pl.multiple_of(x * CELLS, CELLS), CELLS)
+
         def reads():
             for index in range(19):
                 cx, cy, cz = VELOCITY[index]
@@ -237,60 +248,102 @@
                     at = x - cx
                     value = cells[index, pl.ds(pl.multiple_of(at * CELLS, CELLS), CELLS), :]
                 if cy:
-                    s = 0 if cy == 1 else 1
-                    line = edge[s, INWARD[cy].index(index), pl.ds(at, 1), :]
-                    value = jnp.where(row == (0 if cy == 1 else CELLS - 1), line, spin(value, cy, 0))
+                    value = jnp.where(row == (0 if cy == 1 else CELLS - 1), 0.0, spin(value, cy, 0))
                 value = spin(value, cz, 1)
-                if keep:
-                    if known:
-                        nxt[index, rows_of(x), :] = value
-                    else:
-                        nxt[index, pl.ds(pl.multiple_of(x * CELLS, CELLS), CELLS), :] = value
-                yield value
+                yield index, value
 
         density, momentum = moments(reads())
-        at = pl.ds(x % FRAME if known else x, 1)
-        if keep:
-            dens[0, x] = density
-        for axis in range(3):
-            speed = momentum[axis] / density
-            if keep:
-                dens[1 + axis, x] = momentum[axis]
-            vel[axis, x + 2] = speed
-            lines[0, axis, at, :] = speed[0:1]
-            lines[1, axis, at, :] = speed[CELLS - 1 : CELLS]
+        sums[0, here, :] = density
+        for axis in range(3):
+            sums[1 + axis, here, :] = momentum[axis]
+            vel[axis, here, :] = momentum[axis] / density
 
     for x in (-2, -1, 0, CELLS - 1, CELLS, CELLS + 1):
-        column(x, True, 0 <= x < CELLS)
+        one(x, True)
 
     @pl.loop(1, CELLS - 1)
     def _(x):
-        column(x, False, True)
+        one(x, False)
+
+    def start(x):
+        return pl.ds(pl.multiple_of(lax.rem(x + FRAME, FRAME) * CELLS, CELLS), CELLS)
 
     @pl.loop(0, 20, unroll=4)
     def _(j):
-        at = pl.ds(lax.rem(j + 22, FRAME), 1)
-        for axis in range(3):
-            value = vel[axis, j]
-            before = jnp.where(row == 0, strip[0, 0, axis, at, :], spin(value, 1, 0))
-            after = jnp.where(row == CELLS - 1, strip[1, 0, axis, at, :], spin(value, -1, 0))
-            tall[axis, j] = 0.5 * value + 0.25 * (before + after)
+        for axis in range(3):
+            value = vel[axis, start(j - 2), :]
+            tall[axis, j] = 0.5 * value + 0.25 * (spin(value, 1, 0) + spin(value, -1, 0))
 
     @pl.loop(0, 18, unroll=3)
     def _(j):
         for axis in range(3):
-            value = 0.5 * tall[axis, j + 1] + 0.25 * (tall[axis, j] + tall[axis, j + 2])
-            high, low = split(value)
-            smooth[axis, j, :, :DEPTH] = high
-            smooth[axis, j, :, DEPTH:] = low
-
+            smooth[axis, start(j - 1), :] = 0.5 * tall[axis, j + 1] + 0.25 * (
+                tall[axis, j] + tall[axis, j + 2]
+            )
+
+
+def step_kernel(
+    cells_far, sums, vel, almost, share, xlow, xhigh, ylow, yhigh, own_x, own_y, own_z, own_riser, table,
+    nxt_far, push, field_far,
+    wide, nxt, field, edge, lines, tall, smooth, dens, impulse, sems,
+):
+    f32, bf16 = jnp.float32, jnp.bfloat16
+    rate = 1.0 / RELAX
+    gain = 1.0 - 0.5 / RELAX
+    row = lax.broadcasted_iota(jnp.int32, (CELLS, DEPTH), 0)
     place = lax.broadcasted_iota(jnp.int32, (FRAME, DEPTH), 0)
     inside = (place <= CELLS) | (place == FRAME - 1)
+    last = (FRAME - 1) * CELLS
+    fetch = pltpu.make_async_copy(
+        cells_far, wide.at[:, pl.ds(CELLS, CELLS * CELLS), :], sems.at[8]
+    )
+    fetch.start()
+    for message, toward in ((xlow, 1), (xhigh, -1)):
+        column = 0 if toward == 1 else CELLS + 1
+        for index in range(19):
+            if VELOCITY[index][0] == toward:
+                here = slice(column * CELLS, (column + 1) * CELLS)
+                wide[index, here, :] = decode(message[PLACE[0, toward][1, index]], index)
+    dens[...] = sums[:, : CELLS * CELLS, :]
+    smooth[:, : (CELLS + 1) * CELLS, :] = almost[:, : (CELLS + 1) * CELLS, :]
+    smooth[:, last:, :] = almost[:, last:, :]
+
+    def over_x(value):
+        return 0.5 * value + 0.25 * (spin(value, 1, 0) + spin(value, -1, 0))
+
     rim = [[], []]
-    for s in range(2):
-        for axis in range(3):
-            value = 0.5 * strip[s, 0, axis] + 0.25 * (strip[s, 1, axis] + lines[s, axis])
-            value = 0.5 * value + 0.25 * (spin(value, 1, 0) + spin(value, -1, 0))
+    for s, (toward, message) in enumerate(((1, ylow), (-1, yhigh))):
+        first = 0 if toward == 1 else CELLS - 1
+
+        def crossing():
+            for n, index in enumerate(INWARD[toward]):
+                cx, _, cz = VELOCITY[index]
+                value = spin(spin(decode(message[n], index), cx, 0), cz, 1)
+                edge[s, n] = value
+                yield index, value
+
+        density, momentum = moments(crossing())
+        whole = []
+        for k, value in enumerate([density, *momentum]):
+            value = value + sums[k, pl.ds(first, FRAME, stride=CELLS), :]
+            dens[k, pl.ds(first, CELLS, stride=CELLS), :] = value[:CELLS]
+            whole.append(value)
+        sent = [
+            message[INTO + 2 * k].astype(f32) + message[INTO + 2 * k + 1].astype(f32)
+            for k in range(SUMS)
+        ]
+        outer = [sent[3 + k] + share[s, k] for k in range(4)]
+        for axis in range(3):
+            beyond = outer[1 + axis] / outer[0]
+            at_edge = whole[1 + axis] / whole[0]
+            second = pl.ds(first + toward, FRAME, stride=CELLS)
+            third = pl.ds(first + 2 * toward, FRAME, stride=CELLS)
+            inner = vel[axis, second, :]
+            smooth[axis, pl.ds(first, FRAME, stride=CELLS), :] = over_x(
+                0.5 * at_edge + 0.25 * (beyond + inner)
+            )
+            smooth[axis, second, :] = over_x(0.5 * inner + 0.25 * (at_edge + vel[axis, third, :]))
+            value = over_x(0.5 * beyond + 0.25 * (sent[axis] + at_edge))
             rim[s].append(jnp.where(inside, value, 0.0))
 
     goal = jnp.concatenate(split(table[...].T), axis=1)
@@ -347,8 +400,11 @@
         at = attr * 4 + 2 * n
         return jnp.concatenate([slab[at : at + 1, :], slab[at + 1 : at + 2, :]], axis=1)
 
-    inner = [smooth[axis, 1 : CELLS + 1].reshape(CELLS * CELLS, 2 * DEPTH) for axis in range(3)]
-    sources = jnp.concatenate([goal, *inner], axis=0)
+    def halves_of(axis, column, count):
+        value = smooth[axis, column * CELLS : (column + count) * CELLS, :]
+        return jnp.concatenate(split(value), axis=1)
+
+    sources = jnp.concatenate([goal, *(halves_of(axis, 0, CELLS) for axis in range(3))], axis=0)
     total = None
     for n in range(MARKS // step):
         here = slice(n * step, (n + 1) * step)
@@ -377,7 +433,8 @@
             CELLS, CELLS, DEPTH
         )
     for message, at, spot_x in ((xlow, CELLS - 1, 0), (xhigh, 0, CELLS + 1)):
-        sources = jnp.concatenate([goal, *(smooth[axis, spot_x] for axis in range(3))], axis=0)
+        column = (spot_x - 1) % FRAME
+        sources = jnp.concatenate([goal, *(halves_of(axis, column, 1) for axis in range(3))], axis=0)
         slab = message[SLABS].astype(f32)
         total = None
         for n in range(MARKS // step):
@@ -393,7 +450,7 @@
         sources = jnp.concatenate([goal, *halves], axis=0)
         total = None
         for tile in range(3):
-            slab = message[SLABS + tile].astype(f32)
+            slab = message[YSLABS + tile].astype(f32)
             for n in range(MARKS // step):
                 mx, my, mz, riser = (take(slab, attr, n) for attr in range(4))
                 keep = my == at
@@ -417,25 +474,31 @@
             after = jnp.where(row == CELLS - 1, lines[1, axis, at, :], spin(value, -1, 0))
             tall[axis, j] = 0.5 * value + 0.25 * (before + after)
 
-    rate = 1.0 / RELAX
-    gain = 1.0 - 0.5 / RELAX
+    def streamed(x, index):
+        cx, cy, cz = VELOCITY[index]
+        start = pl.multiple_of((x + (1 - cx)) * CELLS, CELLS)
+        value = spin(spin(wide[index, pl.ds(start, CELLS), :], cy, 0), cz, 1)
+        if cy:
+            line = edge[0 if cy == 1 else 1, INWARD[cy].index(index), pl.ds(x, 1), :]
+            value = jnp.where(row == (0 if cy == 1 else CELLS - 1), line, value)
+        return (1.0 - rate) * value
 
     def collide(x):
-        density = dens[0, x]
+        at = pl.ds(pl.multiple_of(x * CELLS, CELLS), CELLS)
+        density = dens[0, at, :]
         own, speed = [], []
         for axis in range(3):
             value = 0.5 * tall[axis, x + 1] + 0.25 * (tall[axis, x] + tall[axis, x + 2])
             field[axis, x] = value
             own.append(value)
-            speed.append((dens[1 + axis, x] + 0.5 * value) / density)
+            speed.append((dens[1 + axis, at, :] + 0.5 * value) / density)
         square = speed[0] * speed[0] + speed[1] * speed[1] + speed[2] * speed[2]
         work = speed[0] * own[0] + speed[1] * own[1] + speed[2] * own[2]
         base = rate * density * (1.0 - 1.5 * square) - 3.0 * gain * work
         flow = [density * value for value in speed]
         even = [4.5 * rate * a + 9.0 * gain * b for a, b in zip(flow, own)]
         odd = [3.0 * rate * a + 3.0 * gain * b for a, b in zip(flow, own)]
-        at = pl.ds(pl.multiple_of(x * CELLS, CELLS), CELLS)
-        nxt[0, at, :] = (1.0 - rate) * nxt[0, at, :] + WEIGHT[0] * base
+        nxt[0, at, :] = streamed(x, 0) + WEIGHT[0] * base
         for weight, indices in ((WEIGHT[1], (1, 3, 5)), (WEIGHT[7], (7, 9, 11, 13, 15, 17))):
             scaled = weight * base
             wide_even = [weight * value for value in even]
@@ -444,14 +507,15 @@
                 direction = VELOCITY[index]
                 both = scaled + along(speed, direction) * along(wide_even, direction)
                 apart = along(wide_odd, direction)
-                nxt[index, at, :] = (1.0 - rate) * nxt[index, at, :] + (both + apart)
-                nxt[index + 1, at, :] = (1.0 - rate) * nxt[index + 1, at, :] + (both - apart)
-
+                nxt[index, at, :] = streamed(x, index) + (both + apart)
+                nxt[index + 1, at, :] = streamed(x, index + 1) + (both - apart)
+
+    fetch.wait()
     copies = []
     chunk = 4
     for n in range(CELLS // chunk):
 
-        @pl.loop(n * chunk, (n + 1) * chunk)
+        @pl.loop(n * chunk, (n + 1) * chunk, unroll=2)
         def _(x):
             collide(x)
 
@@ -477,7 +541,7 @@
     modes = panel.shape[1]
     vmem = pl.BlockSpec(memory_space=pltpu.VMEM)
     face = shape((SLABS + 1, CELLS, DEPTH), bf16)
-    strip = shape((SLABS + 3, FRAME, DEPTH), bf16)
+    strip = shape((YSLABS + 3, FRAME, DEPTH), bf16)
 
     def limit(mib):
         return pltpu.CompilerParams(vmem_limit_bytes=mib << 20)
@@ -521,6 +585,23 @@
     )(cells, xlow, xhigh, *marks)
     ylow = lax.ppermute(yup, "gy", ring("gy", 1))
     yhigh = lax.ppermute(ydown, "gy", ring("gy", -1))
+    early = pl.pallas_call(
+        columns,
+        out_shape=(
+            shape((4, FRAME * CELLS, DEPTH), f32),
+            shape((3, FRAME * CELLS, DEPTH), f32),
+            shape((3, FRAME * CELLS, DEPTH), f32),
+            shape((2, 4, FRAME, DEPTH), f32),
+        ),
+        in_specs=[vmem] * 3,
+        out_specs=(vmem,) * 4,
+        scratch_shapes=[
+            pltpu.VMEM((19, 8 * CELLS, DEPTH), f32),
+            pltpu.VMEM((3, 20, CELLS, DEPTH), f32),
+        ],
+        compiler_params=limit(12),
+        name="columns",
+    )(cells, xlow, xhigh)
     nxt, push, field = pl.pallas_call(
         step_kernel,
         out_shape=(
@@ -528,25 +609,23 @@
             shape((3, 1, MARKS), f32),
             shape((3, CELLS, CELLS, DEPTH), f32),
         ),
-        in_specs=[vmem] * 10,
+        in_specs=[anywhere] + [vmem] * 13,
         out_specs=(anywhere, vmem, anywhere),
         scratch_shapes=[
+            pltpu.VMEM((19, (CELLS + 2) * CELLS, DEPTH), f32),
             pltpu.VMEM((19, CELLS * CELLS, DEPTH), f32),
             pltpu.VMEM((3, CELLS, CELLS, DEPTH), f32),
-            pltpu.VMEM((19, 8 * CELLS, DEPTH), f32),
-            pltpu.VMEM((2, 5, FRAME, DEPTH), f32),
-            pltpu.VMEM((2, 2, 3, FRAME, DEPTH), f32),
+            pltpu.VMEM((2, INTO, FRAME, DEPTH), f32),
             pltpu.VMEM((2, 3, FRAME, DEPTH), f32),
-            pltpu.VMEM((3, 20, CELLS, DEPTH), f32),
-            pltpu.VMEM((3, 20, CELLS, DEPTH), f32),
-            pltpu.VMEM((3, 18, CELLS, 2 * DEPTH), bf16),
-            pltpu.VMEM((4, CELLS, CELLS, DEPTH), f32),
             pltpu.VMEM((3, 18, CELLS, DEPTH), f32),
-            pltpu.SemaphoreType.DMA((8,)),
+            pltpu.VMEM((3, FRAME * CELLS, DEPTH), f32),
+            pltpu.VMEM((4, CELLS * CELLS, DEPTH), f32),
+            pltpu.VMEM((3, 18, CELLS, DEPTH), f32),
+            pltpu.SemaphoreType.DMA((9,)),
         ],
-        compiler_params=limit(32),
+        compiler_params=limit(60),
         name="step_kernel",
-    )(cells, xlow, xhigh, ylow, yhigh, *marks, table)
+    )(cells, *early, xlow, xhigh, ylow, yhigh, *marks, table)
     return (
         nxt.reshape(19, CELLS, CELLS, DEPTH),
         push.transpose(1, 0, 2)[None],

time: 41.2 us -> 42.1 us (1.022)
  blocking collectives: 18.5 us -> 0 us
  starting transfers between devices: 6.9 us -> 15.9 us
  waiting for transfers between devices: 5.21 us -> 9.72 us
  local copies, waits for them, and re-layouts: 0.03 us -> 3.94 us
  Pallas kernels: 9.77 us -> 11.6 us
    all_to_all x1 -> x0, blocking collectives: 18.5 us -> none  [on_device(): table = lax.all_to_all(rows, ('gx', 'gy'), 0, 0, tiled=True)]
    all_to_all x0 -> x1, starting transfers between devices: none -> 9.03 us  [on_device(): table = lax.all_to_all(rows, ('gx', 'gy'), 0, 0, tiled=True)]
    all_to_all x0 -> x1, waiting for transfers between devices: none -> 4.52 us  [on_device(): table = lax.all_to_all(rows, ('gx', 'gy'), 0, 0, tiled=True)]
    unnamed x12 -> x28, local copies, waits for them, and re-layouts: 0.03 us -> 3.94 us
    pallas_call x0 -> x1, Pallas kernels: none -> 1.88 us  [on_device(): pl.pallas_call(columns, out_shape=(shape((4, FRAME * CELLS, DEPTH), f32),...]
  transfers between devices with their start and end apart: 4 -> 5, of which waited for: 2 -> 3; matrix products, arithmetic and copies ran while one was open for 0% -> 0% of each run, Pallas kernels for 0% -> 4%
where the time goes in v2:
time: 42.1 us; the launch traced here: 41.9 us
  starting transfers between devices  15.9 us (38%)
  Pallas kernels  11.6 us (28%)
  waiting for transfers between devices  9.72 us (23%)
  local copies, waits for them, and re-layouts  3.94 us (9%)
  between operations  0.77 us (2%)
    all_to_all x1, starting transfers between devices, on_device(): table = lax.all_to_all(rows, ('gx', 'gy'), 0, 0, tiled=True)  9.03 us
    pallas_call x1, Pallas kernels, on_device(): pl.pallas_call(step_kernel, out_shape=(shape((19, CELLS * CELLS, DEPTH),...  6.95 us
    all_to_all x1, waiting for transfers between devices, on_device(): table = lax.all_to_all(rows, ('gx', 'gy'), 0, 0, tiled=True)  4.52 us
    unnamed x28, local copies, waits for them, and re-layouts  3.94 us
    ppermute x1, starting transfers between devices, on_device(): xlow = lax.ppermute(xup, 'gx', ring('gx', 1))  3.08 us
    ppermute x1, waiting for transfers between devices, on_device(): xhigh = lax.ppermute(xdown, 'gx', ring('gx', -1))  2.67 us
    ppermute x1, waiting for transfers between devices, on_device(): xlow = lax.ppermute(xup, 'gx', ring('gx', 1))  2.53 us
    ppermute x1, starting transfers between devices, on_device(): yhigh = lax.ppermute(ydown, 'gy', ring('gy', -1))  2.45 us
  transfers between devices with their start and end apart: 5, of which 3 were waited for; matrix products, arithmetic and copies ran while one was open for 0% of the time, Pallas kernels for 4%

profile of v2, /device:TPU:1, one launch (start us, length us, event | category | flops | bytes accessed | tf_op | source)
XLA Modules:
  0.0 41.9 jit_solution(4971227206879674520)
XLA Ops:
  0.6 0.0 copy-start.10
  0.6 0.0 copy-start.9
  0.7 0.0 copy-start.8
  0.7 0.0 copy-start.7
  0.7 0.0 copy-start
  0.7 2.3 %pack_x.1 = (bf16[39,16,128]{2,1,0:T(8,128)(2,1)}, bf16[39,16,128]{2,1,0:T(8,128)(2,1)}, f32[128,128]{1,0:T(8,128)}) custom-call(f32[19,256,128]{2,1,0:T(8,128)} %bitcast.14, s32[1,512]{1,0:T(1,128)} %bitcast.18, s32[1,512]{1,0:T(1,128)} %bitcast.21, s32[1,512]{1,0:T(1,128)} %bitcast.24, s32[1,512]{1,0:T(1,128)} %bitcast.27, bf16[64,200]{1,0:T(8,128)(2,1)} %bitcast.31, ...), custom_call_target="tpu_custom_call" | custom-call | tf_op jit(solution)/shard_map/pack_x/pallas_call | solution.py:550
  3.0 3.1 %collective-permute-start = (bf16[39,16,128]{2,1,0:T(8,128)(2,1)}, bf16[39,16,128]{2,1,0:T(8,128)(2,1)S(1)}, u32[]{:S(2)}, u32[]{:S(2)}) collective-permute-start(bf16[39,16,128]{2,1,0:T(8,128)(2,1)} %get-tuple-element.15), channel_id=1, source_target_pairs={{0,8},{8,16},{16,24},{24,32},{32,40},{40,48},{48,56},{56,64},{64,7... | collective-permute-start | bytes 479240 | tf_op jit(solution)/shard_map/ppermute | solution.py:571
  6.1 0.0 collective-permute-start.1
  6.1 2.5 %collective-permute-done.xlow = bf16[39,16,128]{2,1,0:T(8,128)(2,1)S(1)} collective-permute-done((bf16[39,16,128]{2,1,0:T(8,128)(2,1)}, bf16[39,16,128]{2,1,0:T(8,128)(2,1)S(1)}, u32[]{:S(2)}, u32[]{:S(2)}) %collective-permute-start) | collective-permute-done | bytes 159776 | tf_op jit(solution)/shard_map/ppermute | solution.py:571
  8.6 0.0 copy-start.1
  8.6 2.7 %collective-permute-done.1.xhigh = bf16[39,16,128]{2,1,0:T(8,128)(2,1)S(1)} collective-permute-done((bf16[39,16,128]{2,1,0:T(8,128)(2,1)}, bf16[39,16,128]{2,1,0:T(8,128)(2,1)S(1)}, u32[]{:S(2)}, u32[]{:S(2)}) %collective-permute-start.1) | collective-permute-done | bytes 159776 | tf_op jit(solution)/shard_map/ppermute | solution.py:572
  11.3 0.0 copy-done.10
  11.3 0.0 copy-done.9
  11.3 0.0 copy-done.8
  11.3 0.0 copy-done.7
  11.3 0.0 copy-done
  11.3 0.0 copy-start.2
  11.3 0.4 %pack_y.1 = (bf16[22,24,128]{2,1,0:T(8,128)(2,1)S(1)}, bf16[22,24,128]{2,1,0:T(8,128)(2,1)S(1)}) custom-call(f32[19,256,128]{2,1,0:T(8,128)S(1)} %bitcast.16, bf16[39,16,128]{2,1,0:T(8,128)(2,1)S(1)} %collective-permute-done.xlow, bf16[39,16,128]{2,1,0:T(8,128)(2,1)S(1)} %collective-permute-done.1.xhigh, s32[1,512]{1,0:T(1,128)S(1)} %bitcast.20, ...), custom_call_target="tpu_custom_call" | custom-call | tf_op jit(solution)/shard_map/pack_y/pallas_call | solution.py:574
  11.8 1.4 %collective-permute-start.2 = (bf16[22,24,128]{2,1,0:T(8,128)(2,1)S(1)}, bf16[22,24,128]{2,1,0:T(8,128)(2,1)S(1)}, u32[]{:S(2)}, u32[]{:S(2)}) collective-permute-start(bf16[22,24,128]{2,1,0:T(8,128)(2,1)S(1)} %get-tuple-element.21), channel_id=1, source_target_pairs={{0,1},{1,2},{2,3},{3,4},{4,5},{5,6},{6,7},{7,0},{8,9},{9,10},{10,1... | collective-permute-start | bytes 405512 | tf_op jit(solution)/shard_map/ppermute | solution.py:586
  13.1 2.4 %collective-permute-start.3 = (bf16[22,24,128]{2,1,0:T(8,128)(2,1)S(1)}, bf16[22,24,128]{2,1,0:T(8,128)(2,1)S(1)}, u32[]{:S(2)}, u32[]{:S(2)}) collective-permute-start(bf16[22,24,128]{2,1,0:T(8,128)(2,1)S(1)} %get-tuple-element.22), channel_id=1, source_target_pairs={{0,7},{1,0},{2,1},{3,2},{4,3},{5,4},{6,5},{7,6},{8,15},{9,8},{10,9... | collective-permute-start | bytes 405512 | tf_op jit(solution)/shard_map/ppermute | solution.py:587
  15.6 9.0 %all-to-all-start = ((f32[128,1,128]{2,1,0:T(1,128)}), f32[128,1,128]{2,1,0:T(1,128)S(1)}, u32[]{:S(2)}, u32[]{:S(2)}) async-start(f32[128,1,128]{2,1,0:T(1,128)} %bitcast.7), calls=%async_computation | async-start | bytes 131072 | tf_op jit(solution)/shard_map/all_to_all | solution.py:573
  24.6 1.9 %columns.1 = (f32[4,384,128]{2,1,0:T(8,128)S(1)}, f32[3,384,128]{2,1,0:T(8,128)S(1)}, f32[3,384,128]{2,1,0:T(8,128)S(1)}, f32[2,4,24,128]{3,2,1,0:T(8,128)S(1)}) custom-call(f32[19,256,128]{2,1,0:T(8,128)S(1)} %bitcast.17, bf16[39,16,128]{2,1,0:T(8,128)(2,1)S(1)} %collective-permute-done.xlow, bf16[39,16,128]{2,1,0:T(8,128)(2,1)S(1)} %collective-permute-done.1.xhigh), custom_call_target="tpu_custom_call" | custom-call | tf_op jit(solution)/shard_map/columns/pallas_call | solution.py:588
  26.5 0.0 copy-done.1
  26.5 0.0 copy-done.2
  26.5 0.0 copy-start.3
  26.5 0.9 %copy-done.3 = f32[4,384,128]{2,1,0:T(8,128)} copy-done((f32[4,384,128]{2,1,0:T(8,128)}, f32[4,384,128]{2,1,0:T(8,128)S(1)}, u32[]{:S(2)}) %copy-start.3) | copy-done | bytes 786456
  27.4 0.0 copy-start.4
  27.4 0.8 %copy-done.4 = f32[3,384,128]{2,1,0:T(8,128)} copy-done((f32[3,384,128]{2,1,0:T(8,128)}, f32[3,384,128]{2,1,0:T(8,128)S(1)}, u32[]{:S(2)}) %copy-start.4) | copy-done | bytes 589848
  28.3 0.0 copy-start.5
  28.3 0.8 %copy-done.5 = f32[3,384,128]{2,1,0:T(8,128)} copy-done((f32[3,384,128]{2,1,0:T(8,128)}, f32[3,384,128]{2,1,0:T(8,128)S(1)}, u32[]{:S(2)}) %copy-start.5) | copy-done | bytes 589848
  29.1 0.0 copy-start.6
  29.1 0.6 %copy-done.6 = f32[2,4,24,128]{3,2,1,0:T(8,128)} copy-done((f32[2,4,24,128]{3,2,1,0:T(8,128)}, f32[2,4,24,128]{3,2,1,0:T(8,128)S(1)}, u32[]{:S(2)}) %copy-start.6) | copy-done | bytes 98328
  29.7 4.5 %all-to-all-done = f32[128,1,128]{2,1,0:T(1,128)S(1)} async-done(((f32[128,1,128]{2,1,0:T(1,128)}), f32[128,1,128]{2,1,0:T(1,128)S(1)}, u32[]{:S(2)}, u32[]{:S(2)}) %all-to-all-start) | async-done | bytes 65568 | tf_op jit(solution)/shard_map/all_to_all | solution.py:573
  34.2 0.0 copy-start.11
  34.2 0.0 collective-permute-done.2.ylow
  34.2 0.0 copy-start.12
  34.2 0.0 collective-permute-done.3.yhigh
  34.2 0.0 copy-start.13
  34.3 0.6 %copy-done.11 = f32[128,1,128]{2,1,0:T(1,128)} copy-done((f32[128,1,128]{2,1,0:T(1,128)}, f32[128,1,128]{2,1,0:T(1,128)S(1)}, u32[]{:S(2)}) %copy-start.11) | copy-done | bytes 65560
  34.9 0.1 copy-done.12
  34.9 0.0 copy-done.13
  35.0 7.0 %step_kernel.1 = (f32[19,256,128]{2,1,0:T(8,128)}, f32[3,1,512]{2,1,0:T(1,128)}, f32[3,16,16,128]{3,2,1,0:T(8,128)}) custom-call(f32[19,256,128]{2,1,0:T(8,128)} %bitcast.15, f32[4,384,128]{2,1,0:T(8,128)} %copy-done.3, f32[3,384,128]{2,1,0:T(8,128)} %copy-done.4, f32[3,384,128]{2,1,0:T(8,128)} %copy-done.5, f32[2,4,24,128]{3,2,1,0:T(8,128)} %copy-done.6, ...), custom_call_target="tpu_custom_call" | custom-call | tf_op jit(solution)/shard_map/step_kernel/pallas_call | solution.py:605
Async XLA Ops:
  0.6 10.6 %copy-start.10 = (s32[1,1,512]{2,1,0:T(1,128)S(1)}, s32[1,1,512]{2,1,0:T(1,128)}, u32[]{:S(2)}) copy-start(s32[1,1,512]{2,1,0:T(1,128)} %param.13) | copy-start | bytes 6148
  0.6 10.6 %copy-start.9 = (s32[1,1,512]{2,1,0:T(1,128)S(1)}, s32[1,1,512]{2,1,0:T(1,128)}, u32[]{:S(2)}) copy-start(s32[1,1,512]{2,1,0:T(1,128)} %param.12) | copy-start | bytes 6148
  0.7 10.6 %copy-start.8 = (s32[1,1,512]{2,1,0:T(1,128)S(1)}, s32[1,1,512]{2,1,0:T(1,128)}, u32[]{:S(2)}) copy-start(s32[1,1,512]{2,1,0:T(1,128)} %param.11) | copy-start | bytes 6148
  0.7 10.6 %copy-start.7 = (s32[1,1,512]{2,1,0:T(1,128)S(1)}, s32[1,1,512]{2,1,0:T(1,128)}, u32[]{:S(2)}) copy-start(s32[1,1,512]{2,1,0:T(1,128)} %param.10) | copy-start | bytes 6148
  0.7 10.6 %copy-start = (f32[19,16,16,128]{3,2,1,0:T(8,128)S(1)}, f32[19,16,16,128]{3,2,1,0:T(8,128)}, u32[]{:S(2)}) copy-start(f32[19,16,16,128]{3,2,1,0:T(8,128)} %param.7) | copy-start | bytes 7471108
  3.0 5.6 %collective-permute-start = (bf16[39,16,128]{2,1,0:T(8,128)(2,1)}, bf16[39,16,128]{2,1,0:T(8,128)(2,1)S(1)}, u32[]{:S(2)}, u32[]{:S(2)}) collective-permute-start(bf16[39,16,128]{2,1,0:T(8,128)(2,1)} %get-tuple-element.15), channel_id=1, source_target_pairs={{0,8},{8,16},{16,24},{24,32},{32,40},{40,48},{48,56},{56,64},{64,7... | collective-permute-start | bytes 479240 | tf_op jit(solution)/shard_map/ppermute | solution.py:571
  6.1 5.2 %collective-permute-start.1 = (bf16[39,16,128]{2,1,0:T(8,128)(2,1)}, bf16[39,16,128]{2,1,0:T(8,128)(2,1)S(1)}, u32[]{:S(2)}, u32[]{:S(2)}) collective-permute-start(bf16[39,16,128]{2,1,0:T(8,128)(2,1)} %get-tuple-element.16), channel_id=1, source_target_pairs={{0,120},{8,0},{16,8},{24,16},{32,24},{40,32},{48,40},{56,48},{64,5... | collective-permute-start | bytes 479240 | tf_op jit(solution)/shard_map/ppermute | solution.py:572
  8.6 17.9 %copy-start.1 = (bf16[39,16,128]{2,1,0:T(8,128)(2,1)}, bf16[39,16,128]{2,1,0:T(8,128)(2,1)S(1)}, u32[]{:S(2)}) copy-start(bf16[39,16,128]{2,1,0:T(8,128)(2,1)S(1)} %collective-permute-done.xlow) | copy-start | bytes 479236
  11.3 15.2 %copy-start.2 = (bf16[39,16,128]{2,1,0:T(8,128)(2,1)}, bf16[39,16,128]{2,1,0:T(8,128)(2,1)S(1)}, u32[]{:S(2)}) copy-start(bf16[39,16,128]{2,1,0:T(8,128)(2,1)S(1)} %collective-permute-done.1.xhigh) | copy-start | bytes 479236
  11.8 22.5 %collective-permute-start.2 = (bf16[22,24,128]{2,1,0:T(8,128)(2,1)S(1)}, bf16[22,24,128]{2,1,0:T(8,128)(2,1)S(1)}, u32[]{:S(2)}, u32[]{:S(2)}) collective-permute-start(bf16[22,24,128]{2,1,0:T(8,128)(2,1)S(1)} %get-tuple-element.21), channel_id=1, source_target_pairs={{0,1},{1,2},{2,3},{3,4},{4,5},{5,6},{6,7},{7,0},{8,9},{9,10},{10,1... | collective-permute-start | bytes 405512 | tf_op jit(solution)/shard_map/ppermute | solution.py:586
  13.1 21.1 %collective-permute-start.3 = (bf16[22,24,128]{2,1,0:T(8,128)(2,1)S(1)}, bf16[22,24,128]{2,1,0:T(8,128)(2,1)S(1)}, u32[]{:S(2)}, u32[]{:S(2)}) collective-permute-start(bf16[22,24,128]{2,1,0:T(8,128)(2,1)S(1)} %get-tuple-element.22), channel_id=1, source_target_pairs={{0,7},{1,0},{2,1},{3,2},{4,3},{5,4},{6,5},{7,6},{8,15},{9,8},{10,9... | collective-permute-start | bytes 405512 | tf_op jit(solution)/shard_map/ppermute | solution.py:587
  15.6 18.7 %all-to-all-start = ((f32[128,1,128]{2,1,0:T(1,128)}), f32[128,1,128]{2,1,0:T(1,128)S(1)}, u32[]{:S(2)}, u32[]{:S(2)}) async-start(f32[128,1,128]{2,1,0:T(1,128)} %bitcast.7), calls=%async_computation | async-start | bytes 131072 | tf_op jit(solution)/shard_map/all_to_all | solution.py:573
  26.5 0.9 %copy-start.3 = (f32[4,384,128]{2,1,0:T(8,128)}, f32[4,384,128]{2,1,0:T(8,128)S(1)}, u32[]{:S(2)}) copy-start(f32[4,384,128]{2,1,0:T(8,128)S(1)} %get-tuple-element.17.sums) | copy-start | bytes 2359300
  27.4 0.8 %copy-start.4 = (f32[3,384,128]{2,1,0:T(8,128)}, f32[3,384,128]{2,1,0:T(8,128)S(1)}, u32[]{:S(2)}) copy-start(f32[3,384,128]{2,1,0:T(8,128)S(1)} %get-tuple-element.18.vel) | copy-start | bytes 1769476
  28.3 0.8 %copy-start.5 = (f32[3,384,128]{2,1,0:T(8,128)}, f32[3,384,128]{2,1,0:T(8,128)S(1)}, u32[]{:S(2)}) copy-start(f32[3,384,128]{2,1,0:T(8,128)S(1)} %get-tuple-element.19.almost) | copy-start | bytes 1769476
  29.1 0.6 %copy-start.6 = (f32[2,4,24,128]{3,2,1,0:T(8,128)}, f32[2,4,24,128]{3,2,1,0:T(8,128)S(1)}, u32[]{:S(2)}) copy-start(f32[2,4,24,128]{3,2,1,0:T(8,128)S(1)} %get-tuple-element.20.share) | copy-start | bytes 294916
  34.2 0.6 %copy-start.11 = (f32[128,1,128]{2,1,0:T(1,128)}, f32[128,1,128]{2,1,0:T(1,128)S(1)}, u32[]{:S(2)}) copy-start(f32[128,1,128]{2,1,0:T(1,128)S(1)} %all-to-all-done) | copy-start | bytes 196612
  34.2 0.7 %copy-start.12 = (bf16[22,24,128]{2,1,0:T(8,128)(2,1)}, bf16[22,24,128]{2,1,0:T(8,128)(2,1)S(1)}, u32[]{:S(2)}) copy-start(bf16[22,24,128]{2,1,0:T(8,128)(2,1)S(1)} %collective-permute-done.2.ylow) | copy-start | bytes 405508
  34.2 0.7 %copy-start.13 = (bf16[22,24,128]{2,1,0:T(8,128)(2,1)}, bf16[22,24,128]{2,1,0:T(8,128)(2,1)S(1)}, u32[]{:S(2)}) copy-start(bf16[22,24,128]{2,1,0:T(8,128)(2,1)S(1)} %collective-permute-done.3.yhigh) | copy-start | bytes 405508

commit v3 on v2

--- a/solution.py
+++ b/solution.py
@@ -199,7 +199,17 @@
     return pltpu.roll(value, shift % value.shape[axis], axis) if shift else value
 
 
-def columns(cells, xlow, xhigh, sums, vel, smooth, share, side, tall):
+def views(state):
+    return state.at[pl.ds(0, 4)], state.at[pl.ds(4, 3)], state.at[pl.ds(7, 3)]
+
+
+def share_rows(side, k):
+    return slice((4 * side + k) * FRAME, (4 * side + k + 1) * FRAME)
+
+
+def columns(cells, xlow, xhigh, state, side, tall):
+    sums, vel, smooth = views(state)
+
     def rows_of(column):
         return slice(column * CELLS, (column + 1) * CELLS)
 
@@ -225,7 +235,7 @@
 
         density, momentum = moments(outward())
         for k, value in enumerate([density, *momentum]):
-            share[s, k] = value
+            state[10, share_rows(s, k), :] = value
 
     row = lax.broadcasted_iota(jnp.int32, (CELLS, DEPTH), 0)
 
@@ -283,7 +293,7 @@
 
 
 def step_kernel(
-    cells_far, sums, vel, almost, share, xlow, xhigh, ylow, yhigh, own_x, own_y, own_z, own_riser, table,
+    cells_far, state, xlow, xhigh, ylow, yhigh, own_x, own_y, own_z, own_riser, table,
     nxt_far, push, field_far,
     wide, nxt, field, edge, lines, tall, smooth, dens, impulse, sems,
 ):
@@ -294,6 +304,7 @@
     place = lax.broadcasted_iota(jnp.int32, (FRAME, DEPTH), 0)
     inside = (place <= CELLS) | (place == FRAME - 1)
     last = (FRAME - 1) * CELLS
+    sums, vel, almost = views(state)
     fetch = pltpu.make_async_copy(
         cells_far, wide.at[:, pl.ds(CELLS, CELLS * CELLS), :], sems.at[8]
     )
@@ -332,7 +343,7 @@
             message[INTO + 2 * k].astype(f32) + message[INTO + 2 * k + 1].astype(f32)
             for k in range(SUMS)
         ]
-        outer = [sent[3 + k] + share[s, k] for k in range(4)]
+        outer = [sent[3 + k] + state[10, share_rows(s, k), :] for k in range(4)]
         for axis in range(3):
             beyond = outer[1 + axis] / outer[0]
             at_edge = whole[1 + axis] / whole[0]
@@ -587,14 +598,9 @@
     yhigh = lax.ppermute(ydown, "gy", ring("gy", -1))
     early = pl.pallas_call(
         columns,
-        out_shape=(
-            shape((4, FRAME * CELLS, DEPTH), f32),
-            shape((3, FRAME * CELLS, DEPTH), f32),
-            shape((3, FRAME * CELLS, DEPTH), f32),
-            shape((2, 4, FRAME, DEPTH), f32),
-        ),
+        out_shape=shape((11, FRAME * CELLS, DEPTH), f32),
         in_specs=[vmem] * 3,
-        out_specs=(vmem,) * 4,
+        out_specs=vmem,
         scratch_shapes=[
             pltpu.VMEM((19, 8 * CELLS, DEPTH), f32),
             pltpu.VMEM((3, 20, CELLS, DEPTH), f32),
@@ -609,7 +615,7 @@
             shape((3, 1, MARKS), f32),
             shape((3, CELLS, CELLS, DEPTH), f32),
         ),
-        in_specs=[anywhere] + [vmem] * 13,
+        in_specs=[anywhere] + [vmem] * 10,
         out_specs=(anywhere, vmem, anywhere),
         scratch_shapes=[
             pltpu.VMEM((19, (CELLS + 2) * CELLS, DEPTH), f32),
@@ -623,9 +629,9 @@
             pltpu.VMEM((3, 18, CELLS, DEPTH), f32),
             pltpu.SemaphoreType.DMA((9,)),
         ],
-        compiler_params=limit(60),
+        compiler_params=limit(24),
         name="step_kernel",
-    )(cells, *early, xlow, xhigh, ylow, yhigh, *marks, table)
+    )(cells, early, xlow, xhigh, ylow, yhigh, *marks, table)
     return (
         nxt.reshape(19, CELLS, CELLS, DEPTH),
         push.transpose(1, 0, 2)[None],

time: 42.1 us -> 41.4 us (0.983)
  waiting for transfers between devices: 9.72 us -> 11.6 us
  Pallas kernels: 11.6 us -> 10 us
  local copies, waits for them, and re-layouts: 3.94 us -> 2.97 us
    all_to_all x1, waiting for transfers between devices: 4.52 us -> 6.4 us  [on_device(): table = lax.all_to_all(rows, ('gx', 'gy'), 0, 0, tiled=True)]
    pallas_call x1, Pallas kernels: 6.95 us -> 5.44 us  [on_device(): pl.pallas_call(step_kernel, out_shape=(shape((19, CELLS * CELLS, DEPTH),...]
    unnamed x28 -> x14, local copies, waits for them, and re-layouts: 3.94 us -> 2.97 us
  transfers between devices with their start and end apart: 5 -> 5, of which waited for: 3 -> 3; matrix products, arithmetic and copies ran while one was open for 0% -> 0% of each run, Pallas kernels for 4% -> 5%
where the time goes in v3:
time: 41.4 us; the launch traced here: 41.3 us
  starting transfers between devices  15.9 us (38%)
  waiting for transfers between devices  11.6 us (28%)
  Pallas kernels  10 us (24%)
  local copies, waits for them, and re-layouts  2.97 us (7%)
  between operations  0.74 us (2%)
    all_to_all x1, starting transfers between devices, on_device(): table = lax.all_to_all(rows, ('gx', 'gy'), 0, 0, tiled=True)  9.03 us
    all_to_all x1, waiting for transfers between devices, on_device(): table = lax.all_to_all(rows, ('gx', 'gy'), 0, 0, tiled=True)  6.4 us
    pallas_call x1, Pallas kernels, on_device(): pl.pallas_call(step_kernel, out_shape=(shape((19, CELLS * CELLS, DEPTH),...  5.44 us
    ppermute x1, starting transfers between devices, on_device(): xlow = lax.ppermute(xup, 'gx', ring('gx', 1))  3.08 us
    unnamed x14, local copies, waits for them, and re-layouts  2.97 us
    ppermute x1, waiting for transfers between devices, on_device(): xhigh = lax.ppermute(xdown, 'gx', ring('gx', -1))  2.67 us
    ppermute x1, waiting for transfers between devices, on_device(): xlow = lax.ppermute(xup, 'gx', ring('gx', 1))  2.53 us
    ppermute x1, starting transfers between devices, on_device(): yhigh = lax.ppermute(ydown, 'gy', ring('gy', -1))  2.45 us
  transfers between devices with their start and end apart: 5, of which 3 were waited for; matrix products, arithmetic and copies ran while one was open for 0% of the time, Pallas kernels for 5%

profile of v3, /device:TPU:1, one launch (start us, length us, event | category | flops | bytes accessed | tf_op | source)
XLA Modules:
  0.0 41.3 jit_solution(4099165024107292948)
XLA Ops:
  0.6 0.0 copy-start.6
  0.6 0.0 copy-start.5
  0.7 0.0 copy-start.4
  0.7 0.0 copy-start.3
  0.7 0.0 copy-start
  0.7 2.3 %pack_x.1 = (bf16[39,16,128]{2,1,0:T(8,128)(2,1)}, bf16[39,16,128]{2,1,0:T(8,128)(2,1)}, f32[128,128]{1,0:T(8,128)}) custom-call(f32[19,256,128]{2,1,0:T(8,128)} %bitcast.14, s32[1,512]{1,0:T(1,128)} %bitcast.19, s32[1,512]{1,0:T(1,128)} %bitcast.22, s32[1,512]{1,0:T(1,128)} %bitcast.25, s32[1,512]{1,0:T(1,128)} %bitcast.28, bf16[64,200]{1,0:T(8,128)(2,1)} %bitcast.31, ...), custom_call_target="tpu_custom_call" | custom-call | tf_op jit(solution)/shard_map/pack_x/pallas_call | solution.py:561
  3.0 3.1 %collective-permute-start = (bf16[39,16,128]{2,1,0:T(8,128)(2,1)}, bf16[39,16,128]{2,1,0:T(8,128)(2,1)S(1)}, u32[]{:S(2)}, u32[]{:S(2)}) collective-permute-start(bf16[39,16,128]{2,1,0:T(8,128)(2,1)} %get-tuple-element.11), channel_id=1, source_target_pairs={{0,8},{8,16},{16,24},{24,32},{32,40},{40,48},{48,56},{56,64},{64,7... | collective-permute-start | bytes 479240 | tf_op jit(solution)/shard_map/ppermute | solution.py:582
  6.1 0.0 collective-permute-start.1
  6.1 2.5 %collective-permute-done.xlow = bf16[39,16,128]{2,1,0:T(8,128)(2,1)S(1)} collective-permute-done((bf16[39,16,128]{2,1,0:T(8,128)(2,1)}, bf16[39,16,128]{2,1,0:T(8,128)(2,1)S(1)}, u32[]{:S(2)}, u32[]{:S(2)}) %collective-permute-start) | collective-permute-done | bytes 159776 | tf_op jit(solution)/shard_map/ppermute | solution.py:582
  8.6 2.7 %collective-permute-done.1.xhigh = bf16[39,16,128]{2,1,0:T(8,128)(2,1)S(1)} collective-permute-done((bf16[39,16,128]{2,1,0:T(8,128)(2,1)}, bf16[39,16,128]{2,1,0:T(8,128)(2,1)S(1)}, u32[]{:S(2)}, u32[]{:S(2)}) %collective-permute-start.1) | collective-permute-done | bytes 159776 | tf_op jit(solution)/shard_map/ppermute | solution.py:583
  11.3 0.0 copy-done.6
  11.3 0.0 copy-done.5
  11.3 0.0 copy-done.4
  11.3 0.0 copy-done.3
  11.3 0.0 copy-done
  11.3 0.4 %pack_y.1 = (bf16[22,24,128]{2,1,0:T(8,128)(2,1)S(1)}, bf16[22,24,128]{2,1,0:T(8,128)(2,1)S(1)}) custom-call(f32[19,256,128]{2,1,0:T(8,128)S(1)} %bitcast.15, bf16[39,16,128]{2,1,0:T(8,128)(2,1)S(1)} %collective-permute-done.xlow, bf16[39,16,128]{2,1,0:T(8,128)(2,1)S(1)} %collective-permute-done.1.xhigh, s32[1,512]{1,0:T(1,128)S(1)} %bitcast.20, ...), custom_call_target="tpu_custom_call" | custom-call | tf_op jit(solution)/shard_map/pack_y/pallas_call | solution.py:585
  11.7 1.4 %collective-permute-start.2 = (bf16[22,24,128]{2,1,0:T(8,128)(2,1)S(1)}, bf16[22,24,128]{2,1,0:T(8,128)(2,1)S(1)}, u32[]{:S(2)}, u32[]{:S(2)}) collective-permute-start(bf16[22,24,128]{2,1,0:T(8,128)(2,1)S(1)} %get-tuple-element.13), channel_id=1, source_target_pairs={{0,1},{1,2},{2,3},{3,4},{4,5},{5,6},{6,7},{7,0},{8,9},{9,10},{10,1... | collective-permute-start | bytes 405512 | tf_op jit(solution)/shard_map/ppermute | solution.py:597
  13.1 2.4 %collective-permute-start.3 = (bf16[22,24,128]{2,1,0:T(8,128)(2,1)S(1)}, bf16[22,24,128]{2,1,0:T(8,128)(2,1)S(1)}, u32[]{:S(2)}, u32[]{:S(2)}) collective-permute-start(bf16[22,24,128]{2,1,0:T(8,128)(2,1)S(1)} %get-tuple-element.14), channel_id=1, source_target_pairs={{0,7},{1,0},{2,1},{3,2},{4,3},{5,4},{6,5},{7,6},{8,15},{9,8},{10,9... | collective-permute-start | bytes 405512 | tf_op jit(solution)/shard_map/ppermute | solution.py:598
  15.5 9.0 %all-to-all-start = ((f32[128,1,128]{2,1,0:T(1,128)}), f32[128,1,128]{2,1,0:T(1,128)S(1)}, u32[]{:S(2)}, u32[]{:S(2)}) async-start(f32[128,1,128]{2,1,0:T(1,128)} %bitcast.7), calls=%async_computation | async-start | bytes 131072 | tf_op jit(solution)/shard_map/all_to_all | solution.py:584
  24.6 1.9 %columns.1.state = f32[11,384,128]{2,1,0:T(8,128)S(1)} custom-call(f32[19,256,128]{2,1,0:T(8,128)S(1)} %bitcast.16, bf16[39,16,128]{2,1,0:T(8,128)(2,1)S(1)} %collective-permute-done.xlow, bf16[39,16,128]{2,1,0:T(8,128)(2,1)S(1)} %collective-permute-done.1.xhigh), custom_call_target="tpu_custom_call" | custom-call | tf_op jit(solution)/shard_map/columns/pallas_call | solution.py:599
  26.5 0.0 copy-start.1
  26.5 1.3 %copy-done.1 = f32[11,384,128]{2,1,0:T(8,128)} copy-done((f32[11,384,128]{2,1,0:T(8,128)}, f32[11,384,128]{2,1,0:T(8,128)S(1)}, u32[]{:S(2)}) %copy-start.1) | copy-done | bytes 2162712
  27.8 6.4 %all-to-all-done = f32[128,1,128]{2,1,0:T(1,128)S(1)} async-done(((f32[128,1,128]{2,1,0:T(1,128)}), f32[128,1,128]{2,1,0:T(1,128)S(1)}, u32[]{:S(2)}, u32[]{:S(2)}) %all-to-all-start) | async-done | bytes 65568 | tf_op jit(solution)/shard_map/all_to_all | solution.py:584
  34.2 0.0 collective-permute-done.2.ylow
  34.2 0.0 collective-permute-done.3.yhigh
  34.2 0.0 copy-start.2
  34.2 1.6 %copy-done.2 = f32[11,384,128]{2,1,0:T(8,128)S(1)} copy-done((f32[11,384,128]{2,1,0:T(8,128)S(1)}, f32[11,384,128]{2,1,0:T(8,128)}, u32[]{:S(2)}) %copy-start.2) | copy-done | bytes 2162712
  35.8 5.4 %step_kernel.1 = (f32[19,256,128]{2,1,0:T(8,128)}, f32[3,1,512]{2,1,0:T(1,128)}, f32[3,16,16,128]{3,2,1,0:T(8,128)}) custom-call(f32[19,256,128]{2,1,0:T(8,128)S(1)} %bitcast.17, f32[11,384,128]{2,1,0:T(8,128)S(1)} %copy-done.2, bf16[39,16,128]{2,1,0:T(8,128)(2,1)S(1)} %collective-permute-done.xlow, bf16[39,16,128]{2,1,0:T(8,128)(2,1)S(1)} %collective-permute-done.1.xhigh, ...), custom_call_target="tpu_custom_call" | custom-call | tf_op jit(solution)/shard_map/step_kernel/pallas_call | solution.py:611
Async XLA Ops:
  0.6 10.6 %copy-start.6 = (s32[1,1,512]{2,1,0:T(1,128)S(1)}, s32[1,1,512]{2,1,0:T(1,128)}, u32[]{:S(2)}) copy-start(s32[1,1,512]{2,1,0:T(1,128)} %param.13) | copy-start | bytes 6148
  0.6 10.6 %copy-start.5 = (s32[1,1,512]{2,1,0:T(1,128)S(1)}, s32[1,1,512]{2,1,0:T(1,128)}, u32[]{:S(2)}) copy-start(s32[1,1,512]{2,1,0:T(1,128)} %param.12) | copy-start | bytes 6148
  0.7 10.6 %copy-start.4 = (s32[1,1,512]{2,1,0:T(1,128)S(1)}, s32[1,1,512]{2,1,0:T(1,128)}, u32[]{:S(2)}) copy-start(s32[1,1,512]{2,1,0:T(1,128)} %param.11) | copy-start | bytes 6148
  0.7 10.6 %copy-start.3 = (s32[1,1,512]{2,1,0:T(1,128)S(1)}, s32[1,1,512]{2,1,0:T(1,128)}, u32[]{:S(2)}) copy-start(s32[1,1,512]{2,1,0:T(1,128)} %param.10) | copy-start | bytes 6148
  0.7 10.6 %copy-start = (f32[19,16,16,128]{3,2,1,0:T(8,128)S(1)}, f32[19,16,16,128]{3,2,1,0:T(8,128)}, u32[]{:S(2)}) copy-start(f32[19,16,16,128]{3,2,1,0:T(8,128)} %param.7) | copy-start | bytes 7471108
  3.0 5.6 %collective-permute-start = (bf16[39,16,128]{2,1,0:T(8,128)(2,1)}, bf16[39,16,128]{2,1,0:T(8,128)(2,1)S(1)}, u32[]{:S(2)}, u32[]{:S(2)}) collective-permute-start(bf16[39,16,128]{2,1,0:T(8,128)(2,1)} %get-tuple-element.11), channel_id=1, source_target_pairs={{0,8},{8,16},{16,24},{24,32},{32,40},{40,48},{48,56},{56,64},{64,7... | collective-permute-start | bytes 479240 | tf_op jit(solution)/shard_map/ppermute | solution.py:582
  6.1 5.2 %collective-permute-start.1 = (bf16[39,16,128]{2,1,0:T(8,128)(2,1)}, bf16[39,16,128]{2,1,0:T(8,128)(2,1)S(1)}, u32[]{:S(2)}, u32[]{:S(2)}) collective-permute-start(bf16[39,16,128]{2,1,0:T(8,128)(2,1)} %get-tuple-element.12), channel_id=1, source_target_pairs={{0,120},{8,0},{16,8},{24,16},{32,24},{40,32},{48,40},{56,48},{64,5... | collective-permute-start | bytes 479240 | tf_op jit(solution)/shard_map/ppermute | solution.py:583
  11.7 22.5 %collective-permute-start.2 = (bf16[22,24,128]{2,1,0:T(8,128)(2,1)S(1)}, bf16[22,24,128]{2,1,0:T(8,128)(2,1)S(1)}, u32[]{:S(2)}, u32[]{:S(2)}) collective-permute-start(bf16[22,24,128]{2,1,0:T(8,128)(2,1)S(1)} %get-tuple-element.13), channel_id=1, source_target_pairs={{0,1},{1,2},{2,3},{3,4},{4,5},{5,6},{6,7},{7,0},{8,9},{9,10},{10,1... | collective-permute-start | bytes 405512 | tf_op jit(solution)/shard_map/ppermute | solution.py:597
  13.1 21.1 %collective-permute-start.3 = (bf16[22,24,128]{2,1,0:T(8,128)(2,1)S(1)}, bf16[22,24,128]{2,1,0:T(8,128)(2,1)S(1)}, u32[]{:S(2)}, u32[]{:S(2)}) collective-permute-start(bf16[22,24,128]{2,1,0:T(8,128)(2,1)S(1)} %get-tuple-element.14), channel_id=1, source_target_pairs={{0,7},{1,0},{2,1},{3,2},{4,3},{5,4},{6,5},{7,6},{8,15},{9,8},{10,9... | collective-permute-start | bytes 405512 | tf_op jit(solution)/shard_map/ppermute | solution.py:598
  15.5 18.7 %all-to-all-start = ((f32[128,1,128]{2,1,0:T(1,128)}), f32[128,1,128]{2,1,0:T(1,128)S(1)}, u32[]{:S(2)}, u32[]{:S(2)}) async-start(f32[128,1,128]{2,1,0:T(1,128)} %bitcast.7), calls=%async_computation | async-start | bytes 131072 | tf_op jit(solution)/shard_map/all_to_all | solution.py:584
  26.5 1.3 %copy-start.1 = (f32[11,384,128]{2,1,0:T(8,128)}, f32[11,384,128]{2,1,0:T(8,128)S(1)}, u32[]{:S(2)}) copy-start(f32[11,384,128]{2,1,0:T(8,128)S(1)} %columns.1.state) | copy-start | bytes 6488068
  34.2 1.6 %copy-start.2 = (f32[11,384,128]{2,1,0:T(8,128)S(1)}, f32[11,384,128]{2,1,0:T(8,128)}, u32[]{:S(2)}) copy-start(f32[11,384,128]{2,1,0:T(8,128)} %copy-done.1) | copy-start | bytes 6488068
